TPU v7x, 256 devices: a whole 4x4x8 slice. The times are simulated.
256 devices in a mesh: dp: 32 (over x, z), ctx: 8 (over y, core).
Axes of the slice: x: 4, y: 4, z: 8, core: 2. Of those that a mesh axis runs over, the one named last changes fastest.
Arguments:
- hidden: bfloat16 [32, 2048, 4096], P('dp', 'ctx'), may hold values from -6 to 6
- segments: int32 [32, 2048], P('dp', 'ctx'), may hold values from 0 to 15, as said below
- gain: float32 [4096], replicated, may hold values from 0.25 to 1.75
- inv_temp: float32 [], replicated, may hold values from 20 to 50
- positives: int32 [512], P(('dp', 'ctx')), may hold values from 0 to 511, as said below
Outputs:
- grad_hidden: bfloat16 [32, 2048, 4096], P('dp', 'ctx')
- grad_gain: float32 [4096], replicated
- loss: float32 [], replicated
Inputs may be any that keep to these rules, and one draw needn't show every extreme that they name: `segments`: in each sequence the document numbers never fall along positions and every document has one position or more; document 0 covers more than half of the sequence's positions. `positives`: no document is its own positive.
All inputs are finite; a program needn't handle non-finite values.
Results may differ from a plain program's by a relative error of at most 0.0053.
Values may be sent and summed in bfloat16 or wider, within the bound.
A program may use at most 64 MiB of HBM per device.

v0:
```python
import jax
import jax.numpy as jnp
from jax import lax
from jax.sharding import PartitionSpec as P

DOCS_DEV = 2


def normalize_docs(pooled_totals, counts):
    pooled = pooled_totals / counts[:, None]
    rnorm = lax.rsqrt(jnp.sum(pooled * pooled, axis=-1, keepdims=True) + 1e-06)
    return (pooled * rnorm, rnorm)


def body(hidden, segments, gain, inv_temp, positives):
    states = hidden[0].astype(jnp.float32)
    scale_t = lax.rsqrt(jnp.mean(states * states, axis=-1, keepdims=True) + 1e-06)
    normalized_rows = states * scale_t * gain
    ctx_count = lax.axis_size("ctx")
    seq_docs = DOCS_DEV * ctx_count
    document_indicator = (
        segments[0][:, None] == jnp.arange(seq_docs, dtype=jnp.int32)[None, :]
    ).astype(jnp.float32)
    pooled_totals = lax.dot_general(
        document_indicator,
        normalized_rows,
        (((0,), (0,)), ((), ())),
        precision=lax.Precision.HIGHEST,
    )
    counts = jnp.sum(document_indicator, axis=0)
    ctx_rank = lax.axis_index("ctx")
    own_sums, own_counts = (
        lax.psum_scatter(pooled_totals, "ctx", scatter_dimension=0, tiled=True),
        lax.psum_scatter(counts, "ctx", scatter_dimension=0, tiled=True),
    )
    emb_f, rnorm = normalize_docs(own_sums, own_counts)
    emb_own = emb_f.astype(jnp.bfloat16)
    emb_all = lax.all_gather(emb_own, ("dp", "ctx"), axis=0, tiled=True)
    all_docs = emb_all.shape[0]
    row_first = (lax.axis_index("dp") * ctx_count + ctx_rank) * DOCS_DEV
    logits = (
        lax.dot_general(
            emb_own, emb_all, (((1,), (1,)), ((), ())), preferred_element_type=jnp.float32
        )
        * inv_temp
    )
    columns = jnp.arange(all_docs, dtype=jnp.int32)[None, :]
    own_rows = row_first + jnp.arange(DOCS_DEV, dtype=jnp.int32)[:, None]
    pos_mask = (columns == positives[:, None]).astype(jnp.float32)
    logits = jnp.where(columns == own_rows, -1e30, logits)
    top = jnp.max(logits, axis=1, keepdims=True)
    expo = jnp.exp(logits - top)
    total = jnp.sum(expo, axis=1, keepdims=True)
    lse = top[:, 0] + jnp.log(total[:, 0])
    loss_local = jnp.sum(lse - jnp.sum(pos_mask * logits, axis=1)) / all_docs
    gmat = ((expo / total - pos_mask) * (inv_temp / all_docs)).astype(jnp.bfloat16)
    row_grad = jnp.dot(gmat, emb_all, preferred_element_type=jnp.float32)
    grad_rows = lax.all_gather(gmat, ("dp", "ctx"), axis=0, tiled=True)
    grad_cols = lax.dynamic_slice_in_dim(grad_rows, row_first, DOCS_DEV, 1)
    col_grad = lax.dot_general(
        grad_cols, emb_all, (((0,), (0,)), ((), ())), preferred_element_type=jnp.float32
    )
    demb = row_grad + col_grad
    dpool = rnorm * (demb - emb_f * jnp.sum(emb_f * demb, axis=-1, keepdims=True))
    dsum_own = dpool / own_counts[:, None]
    dsum_seq = lax.all_gather(dsum_own, "ctx", axis=0, tiled=True)
    normalized_gradient = jnp.dot(document_indicator, dsum_seq, precision=lax.Precision.HIGHEST)
    gain_local = jnp.sum(normalized_gradient * states * scale_t, axis=0)
    grad_gain, loss = lax.psum((gain_local, loss_local), ("dp", "ctx"))
    grad_out = normalized_gradient * gain
    inner = jnp.mean(grad_out * states, axis=-1, keepdims=True)
    grad_hidden = (scale_t * grad_out - states * scale_t**3 * inner).astype(jnp.bfloat16)
    return (grad_hidden[None], grad_gain, loss)


def solution(mesh):
    return jax.shard_map(
        body,
        mesh=mesh,
        in_specs=(P("dp", "ctx", None), P("dp", "ctx"), P(), P(), P(("dp", "ctx"))),
        out_specs=(P("dp", "ctx", None), P(), P()),
        check_vma=False,
    )
```

profile of v0, /device:TPU:1, one launch (start us, length us, event | category | flops | bytes accessed | tf_op | source)
XLA Modules:
  0.0 389.6 jit_solution(4266364074889755771)
XLA Ops:
  7.2 0.0 copy-start.5
  7.2 0.0 copy-start.4
  7.2 0.0 all-reduce.5.cloned.1.call-start
  7.2 2.1 fusion
  9.3 4.2 %fusion.2 = f32[16,4096]{1,0:T(8,128)} fusion(bf16[1,256,4096]{2,1,0:T(8,128)(2,1)} %param.5, f32[4096]{0:T(1024)} %param.7, f32[256]{0:T(256)S(1)} %get-tuple-element.12, s32[256]{0:T(256)} %bitcast.26), kind=kOutput, calls=%fused_computation.8 | convolution fusion | flops 204476416 | bytes 2377728 | tf_op jit(solution)/shard_map/dot_general | solution.py:24
  13.5 0.0 all-reduce.5.cloned.1.call-update
  13.5 0.0 all-gather.5.cloned.1.call-start
  13.6 0.0 copy-done.5
  13.6 0.6 dynamic-slice
  14.8 0.0 copy-done.4
  14.8 0.1 convert_reduce_fusion
  15.0 15.0 %all-reduce.1 = f32[16]{0:T(128)S(1)} all-reduce(f32[16]{0:T(128)S(1)} %convert_reduce_fusion), channel_id=3, replica_groups=mesh['dp'=32,'ctx'=8] {'ctx'}, use_global_device_ids=true, to_apply=%region_3.0.clone | all-reduce | flops 16 | bytes 128
  29.9 0.1 dynamic-slice.3
  30.0 50.8 %all-reduce.5.cloned.1.call-done = f32[16,4096]{1,0:T(8,128)} async-done(((f32[16,4096]{1,0:T(8,128)}), f32[16,4096]{1,0:T(8,128)}) %all-reduce.5.cloned.1.call-update) | async-done | bytes 262160
  80.8 1.1 multiply_reduce_fusion.1
  81.9 0.7 fusion.30
  82.6 0.0 all-gather.5.cloned.1.call-update
  83.3 119.1 %all-gather.5.cloned.1.call-done = bf16[256,2,4096]{2,1,0:T(2,128)(2,1)} async-done(((bf16[1,2,4096]{2,1,0:T(2,128)(2,1)}), bf16[256,2,4096]{2,1,0:T(2,128)(2,1)}) %all-gather.5.cloned.1.call-update) | async-done | bytes 4194320 | tf_op jit(solution)/shard_map/all_gather | solution.py:38
  202.4 7.2 %reshape.46 = bf16[512,4096]{1,0:T(8,128)(2,1)} reshape(bf16[256,2,4096]{2,1,0:T(2,128)(2,1)} %all-gather.5.cloned.1.call-done) | data formatting | bytes 8388608
  209.6 0.0 copy-start.3
  209.6 0.0 copy-start
  209.6 3.6 fusion.21
  213.3 0.0 copy-done.3
  213.3 0.2 select_reduce_fusion
  213.5 0.1 fusion.29
  213.6 0.0 copy-done
  213.6 0.7 fusion.22
  214.3 0.0 copy-start.1
  214.3 0.0 copy-start.2
  214.3 0.6 subtract_reduce_fusion
  215.6 67.0 %all-gather.1 = bf16[256,2,512]{2,1,0:T(2,128)(2,1)S(1)} all-gather(bf16[1,2,512]{2,1,0:T(2,128)(2,1)S(1)} %fusion.29), channel_id=1, replica_groups=mesh['dp'=32,'ctx'=8] {'dp','ctx'}, dimensions={0}, use_global_device_ids=true | all-gather | bytes 526336 | tf_op jit(solution)/shard_map/all_gather | solution.py:58
  282.6 0.2 reshape.48
  282.8 3.1 multiply_reduce_fusion
  285.9 0.1 divide_bitcast_fusion
  286.0 12.8 %all-gather.2 = f32[8,2,4096]{2,1,0:T(2,128)S(1)} all-gather(f32[1,2,4096]{2,1,0:T(2,128)S(1)} %divide_bitcast_fusion), channel_id=1, replica_groups=mesh['dp'=32,'ctx'=8] {'ctx'}, dimensions={0}, use_global_device_ids=true | all-gather | bytes 294912 | tf_op jit(solution)/shard_map/all_gather | solution.py:66
  298.8 0.2 reshape.50
  299.0 0.0 copy-done.1
  299.0 0.0 copy-done.2
  299.0 4.8 %fusion.9 = (f32[4096]{0:T(1024)S(1)}, f32[256]{0:T(256)S(1)}, f32[256,4096]{1,0:T(8,128)}) fusion(bf16[1,256,4096]{2,1,0:T(8,128)(2,1)S(1)} %copy-done.1, f32[256]{0:T(256)S(1)} %get-tuple-element.12, f32[4096]{0:T(1024)S(1)} %copy-done.2, f32[16,4096]{1,0:T(8,128)S(1)} %reshape.50, s32[256]{0:T(256)S(1)} %bitcast.28), kind=kOutput, calls=%fused_computation.14 | convolution fusion | flops 208666368 | bytes 6589440 | tf_op jit(solution)/shard_map/dot_general | solution.py:67
  303.8 74.0 %all-reduce.2 = (f32[4096]{0:T(1024)}, f32[]{:T(128)}) all-reduce(f32[4096]{0:T(1024)S(1)} %get-tuple-element.3, f32[]{:T(128)S(6)} %div.42), channel_id=1, replica_groups=mesh['dp'=32,'ctx'=8] {'dp','ctx'}, use_global_device_ids=true, to_apply=%region_10.11 | all-reduce | flops 4097 | bytes 32776 | tf_op jit(solution)/shard_map/psum | solution.py:69
  377.8 5.0 %fusion.10 = bf16[1,256,4096]{2,1,0:T(8,128)(2,1)} fusion(f32[256,4096]{1,0:T(8,128)} %get-tuple-element.17, bf16[1,256,4096]{2,1,0:T(8,128)(2,1)S(1)} %copy-done.1, f32[256]{0:T(256)S(1)} %broadcast_multiply_fusion, f32[256]{0:T(256)S(1)} %get-tuple-element.11, f32[4096]{0:T(1024)S(1)} %copy-done.2, f32[256]{0:T(256)S(1)} %get-tuple-element.12), kind=kLoop, calls=%fused_computation.15 | loop fusion | flops 7340032 | bytes 8408064 | tf_op jit(solution)/shard_map/broadcast_in_dim | solution.py:73
  (4 shorter events, 0.0 us)
Async XLA Ops:
  7.2 6.4 %copy-start.5 = (u32[256]{0:T(256)S(1)}, u32[256]{0:T(256)}, u32[]{:S(2)}) copy-start(u32[256]{0:T(256)} %constant.40) | copy-start | bytes 3076
  7.2 7.7 %copy-start.4 = (s32[1,256]{1,0:T(1,128)S(1)}, s32[1,256]{1,0:T(1,128)}, u32[]{:S(2)}) copy-start(s32[1,256]{1,0:T(1,128)} %param.6) | copy-start | bytes 3076
  7.2 73.6 %all-reduce.5.cloned.1.call-start = ((), (), s32[]{:S(2)}) async-start(), calls=%async_computation.1 | async-start | bytes 524288
  13.5 188.9 %all-gather.5.cloned.1.call-start = ((), (), s32[]{:S(2)}) async-start(), calls=%async_computation | async-start | bytes 4210688 | tf_op jit(solution)/shard_map/all_gather | solution.py:38
  209.6 3.6 copy-start.3
  209.6 4.0 %copy-start = (bf16[512,4096]{1,0:T(8,128)(2,1)S(1)}, bf16[512,4096]{1,0:T(8,128)(2,1)}, u32[]{:S(2)}) copy-start(bf16[512,4096]{1,0:T(8,128)(2,1)} %reshape.46) | copy-start | bytes 12582916
  214.3 84.7 %copy-start.1 = (bf16[1,256,4096]{2,1,0:T(8,128)(2,1)S(1)}, bf16[1,256,4096]{2,1,0:T(8,128)(2,1)}, u32[]{:S(2)}) copy-start(bf16[1,256,4096]{2,1,0:T(8,128)(2,1)} %param.5) | copy-start | bytes 6291460
  214.3 84.7 %copy-start.2 = (f32[4096]{0:T(1024)S(1)}, f32[4096]{0:T(1024)}, u32[]{:S(2)}) copy-start(f32[4096]{0:T(1024)} %param.7) | copy-start | bytes 49156
Sparse Core Ops, SparseCore 0:
  13.7 67.1 all-reduce.4
  85.1 117.3 all-gather.4
where the time goes:
time: 390 us
  waiting for transfers between devices  170 us (44%)
  blocking collectives  169 us (43%)
  matrix products  16.3 us (4%)
  between operations  16.1 us (4%)
  other arithmetic  10 us (3%)
  local copies, waits for them, and re-layouts  8.27 us (2%)
    all_gather x1, waiting for transfers between devices, body(): emb_all = lax.all_gather(emb_own, ('dp', 'ctx'), axis=0, tiled=True)  119 us
    psum x1, blocking collectives, body(): grad_gain, loss = lax.psum((gain_local, loss_local), ('dp', 'ctx'))  74 us
    all_gather x1, blocking collectives, body(): grad_rows = lax.all_gather(gmat, ('dp', 'ctx'), axis=0, tiled=True)  67 us
    unnamed x3, waiting for transfers between devices  50.8 us
    unnamed x1, blocking collectives  15 us
    all_gather x1, blocking collectives, body(): dsum_seq = lax.all_gather(dsum_own, 'ctx', axis=0, tiled=True)  12.8 us
    unnamed x17, local copies, waits for them, and re-layouts  8.27 us
  transfers between devices with their start and end apart: 2, of which 2 were waited for; matrix products, arithmetic and copies ran while one was open for 0% of the time, Pallas kernels for 0%

commit v1 on v0

v1 whole, which is shorter than its diff:
```python
import functools

import jax
import jax.numpy as jnp
from jax import lax
from jax.experimental import pallas as pl
from jax.experimental.pallas import tpu as pltpu
from jax.sharding import PartitionSpec as P

MESH = pl.DeviceIdType.MESH
F32 = jnp.float32
BF16 = jnp.bfloat16

NX, NY, NZ = 4, 4, 8
N_DP, N_CTX = NX * NZ, NY * 2
DOCS = 16
ALL = N_DP * DOCS
TOK = 256
D = 4096
FB = D // N_CTX
PAIR_ORDER = (0, 1, 3, 2)
RB = 128


def mod(a, n):
    return lax.rem(a, n)


def dot(a, b, dims):
    return lax.dot_general(a, b, (dims, ((), ())), preferred_element_type=F32)


def gather_kernel(
    h_hbm, seg_ref, pos_ref, gain_ref, it_ref,
    gd_ref, oh_ref, sc_ref, gg_ref, loss_ref,
    h, part, recv, emb, meta_own, meta_ctx, meta, gram, nmat, tbuf,
    h_sem, m1_send, m1_recv, mz_send, mz_recv, mx_send, mx_recv, p1_send, p1_recv,
    z_send, z_recv, a_send, a_recv, b_send, b_recv, s_send, s_recv,
):
    dp, ctx = lax.axis_index("dp"), lax.axis_index("ctx")
    x, z = lax.div(dp, NZ), mod(dp, NZ)
    y, c = lax.div(ctx, 2), mod(ctx, 2)
    a = (1 - c) * x + c * y
    b = (1 - c) * y + c * x

    def at_a(aa):
        return ((1 - c) * (aa * NZ + z) + c * dp, (1 - c) * ctx + c * (aa * 2 + c))

    def at_b(bb):
        return ((1 - c) * dp + c * (bb * NZ + z), (1 - c) * (bb * 2 + c) + c * ctx)

    sibling = (dp, ctx + 1 - 2 * c)

    barrier = pltpu.get_barrier_semaphore()
    peers = [(dp, mod(ctx + k, N_CTX)) for k in range(1, N_CTX)]
    peers += [(x * NZ + mod(z + k, NZ), ctx) for k in range(1, NZ)]
    peers += [(mod(x + k, NX) * NZ + z, ctx) for k in range(1, NX)]
    for peer in peers:
        pl.semaphore_signal(barrier, inc=1, device_id=peer, device_id_type=MESH)

    h_copies = []
    for i in range(4):
        rows = pl.ds(i * (TOK // 4), TOK // 4)
        h_copies.append(pltpu.make_async_copy(h_hbm.at[rows], h.at[rows], h_sem.at[i]))
        h_copies[-1].start()

    seg = seg_ref[...]
    doc_rows = lax.broadcasted_iota(jnp.int32, (DOCS, TOK), 0)
    onehot = (seg == doc_rows).astype(F32)
    doc_col = lax.broadcasted_iota(jnp.int32, (DOCS, 128), 0)
    lane = lax.broadcasted_iota(jnp.int32, (DOCS, 128), 1)
    pos = jnp.where(doc_col == 2 * ctx, pos_ref[0], jnp.where(doc_col == 2 * ctx + 1, pos_ref[1], 0))
    meta_own[...] = jnp.where(lane == 0, pos.astype(F32), jnp.sum(onehot, axis=1, keepdims=True))

    squares = []
    for i in range(4):
        h_copies[i].wait()
        acc = jnp.zeros((TOK // 4, 128), F32)
        for j in range(D // 128):
            v = h[i * (TOK // 4):(i + 1) * (TOK // 4), j * 128:(j + 1) * 128].astype(F32)
            acc = acc + v * v
        squares.append(jnp.sum(acc, axis=1, keepdims=True))
    mean_sq = jnp.concatenate(squares, axis=0) * (1.0 / D)
    scale = jnp.broadcast_to(lax.rsqrt(mean_sq + 1e-06), (TOK, 128))
    sc_ref[...] = scale
    weight = onehot * jnp.transpose(scale)[0:DOCS, :]
    w_hi = weight.astype(BF16)
    w_lo = (weight - w_hi.astype(F32)).astype(BF16)
    w2 = jnp.concatenate([w_hi, w_lo], axis=0)
    for j in range(N_CTX):
        cols = slice(j * FB, (j + 1) * FB)
        both = dot(w2, h[:, cols], ((1,), (0,)))
        part[:, cols] = ((both[0:DOCS] + both[DOCS:]) * gain_ref[:, cols]).astype(BF16)

    pl.semaphore_wait(barrier, len(peers))

    def p1(src, dst):
        return pltpu.make_async_remote_copy(
            src_ref=part.at[:, pl.ds(pl.multiple_of(dst * FB, FB), FB)], dst_ref=recv.at[src],
            send_sem=p1_send, recv_sem=p1_recv.at[src], device_id=(dp, dst), device_id_type=MESH,
        )

    def m1(src, dst):
        return pltpu.make_async_remote_copy(
            src_ref=meta_own, dst_ref=meta_ctx.at[src],
            send_sem=m1_send, recv_sem=m1_recv.at[src], device_id=(dp, dst), device_id_type=MESH,
        )

    others = [mod(ctx + k, N_CTX) for k in (4, 5, 3, 2, 6, 7, 1)]
    for other in others:
        p1(ctx, other).start()
    for other in others:
        m1(ctx, other).start()

    my_col = pl.ds(pl.multiple_of(ctx * FB, FB), FB)
    total = part[:, my_col].astype(F32)
    for other in reversed(others):
        p1(other, ctx).wait_recv()
        total = total + recv[other].astype(F32)
    emb[dp, :, my_col] = total.astype(BF16)

    def zcopy(zz, dst):
        ref = emb.at[x * NZ + zz, :, my_col]
        return pltpu.make_async_remote_copy(
            src_ref=ref, dst_ref=ref, send_sem=z_send, recv_sem=z_recv.at[zz],
            device_id=(x * NZ + dst, ctx), device_id_type=MESH,
        )

    for k in (4, 3, 5, 2, 6, 1, 7):
        zcopy(z, mod(z + k, NZ)).start()

    def mz(zz, dst):
        ref = meta.at[x * NZ + zz]
        return pltpu.make_async_remote_copy(
            src_ref=ref, dst_ref=ref, send_sem=mz_send, recv_sem=mz_recv.at[zz],
            device_id=(x * NZ + dst, ctx), device_id_type=MESH,
        )

    def mx(xx, dst):
        ref = meta.at[pl.ds(xx * NZ, NZ)]
        return pltpu.make_async_remote_copy(
            src_ref=ref, dst_ref=ref, send_sem=mx_send, recv_sem=mx_recv.at[xx],
            device_id=(dst * NZ + z, ctx), device_id_type=MESH,
        )

    meta_sum = meta_own[...]
    for other in others:
        m1(other, ctx).wait_recv()
        meta_sum = meta_sum + meta_ctx[other]
    meta[dp] = meta_sum
    for k in range(1, NZ):
        mz(z, mod(z + k, NZ)).start()

    a_off = lambda k: mod(a + k, NX)
    b_off = lambda k: mod(b + k, NX)
    pair_of = lambda k: mod(lax.div(z, 2) + PAIR_ORDER[k], NZ // 2)

    def block(aa, bb, k):
        xx = (1 - c) * aa + c * bb
        yy = (1 - c) * bb + c * aa
        col = pl.multiple_of((yy * 2 + c) * FB, FB)
        return emb.at[pl.ds(xx * NZ + 2 * pair_of(k), 2), :, pl.ds(col, FB)]

    def acopy(aa, k, way, to):
        ref = block(aa, b, k)
        return pltpu.make_async_remote_copy(
            src_ref=ref, dst_ref=ref, send_sem=a_send, recv_sem=a_recv.at[3 * k + way],
            device_id=at_a(to), device_id_type=MESH,
        )

    def bcopy(am, bb, k, way, to):
        ref = block(a_off(am), bb, k)
        return pltpu.make_async_remote_copy(
            src_ref=ref, dst_ref=ref, send_sem=b_send, recv_sem=b_recv.at[12 * k + 3 * am + way],
            device_id=at_b(to), device_id_type=MESH,
        )

    def sib(am, bm, k):
        ref = block(a_off(am), b_off(bm), k)
        return pltpu.make_async_remote_copy(
            src_ref=ref, dst_ref=ref, send_sem=s_send, recv_sem=s_recv,
            device_id=sibling, device_id_type=MESH,
        )

    def a_start(k):
        acopy(a, k, 0, a_off(1)).start()
        acopy(a, k, 1, a_off(3)).start()

    def b_start(am, k):
        bcopy(am, b, k, 0, b_off(1)).start()
        bcopy(am, b, k, 1, b_off(3)).start()
        sib(am, 0, k).start()

    def a_relay(k):
        acopy(a_off(3), k, 0, a).wait_recv()
        acopy(a_off(1), k, 1, a).wait_recv()
        if k % 2 == 0:
            acopy(a_off(3), k, 2, a_off(1)).start()
        else:
            acopy(a_off(1), k, 2, a_off(3)).start()
        b_start(3, k)
        b_start(1, k)

    def a_last(k):
        acopy(a_off(2), k, 2, a).wait_recv()
        b_start(2, k)

    def b_relay(am, k):
        bcopy(am, b_off(3), k, 0, b).wait_recv()
        bcopy(am, b_off(1), k, 1, b).wait_recv()
        if (k + (am == 2)) % 2 == 0:
            bcopy(am, b_off(3), k, 2, b_off(1)).start()
        else:
            bcopy(am, b_off(1), k, 2, b_off(3)).start()
        sib(am, 3, k).start()
        sib(am, 1, k).start()

    def b_last(am, k):
        bcopy(am, b_off(2), k, 2, b).wait_recv()
        sib(am, 2, k).start()

    for t in range(9):
        if t < 4:
            for i in range(2):
                zz = 2 * pair_of(t) + i
                if t == 0:
                    zz = z + 1 - 2 * mod(z, 2)
                    if i == 1:
                        continue
                zcopy(zz, z).wait_recv()
            a_start(t)
            b_start(0, t)
        if 1 <= t < 5:
            a_relay(t - 1)
            b_relay(0, t - 1)
        if 2 <= t < 6:
            a_last(t - 2)
            b_relay(3, t - 2)
            b_relay(1, t - 2)
            b_last(0, t - 2)
        if 3 <= t < 7:
            b_relay(2, t - 3)
            b_last(3, t - 3)
            b_last(1, t - 3)
        if 4 <= t < 8:
            b_last(2, t - 4)
        if t == 3:
            for k in range(1, NZ):
                mz(mod(z + k, NZ), z).wait_recv()
            for k in range(1, NX):
                mx(x, mod(x + k, NX)).start()

    gram[...] = jnp.zeros_like(gram)

    def gram_of(core):
        @pl.loop(0, NY)
        def _(yy):
            col = pl.multiple_of((yy * 2 + core) * FB, FB)
            e = emb[:, :, pl.ds(col, FB)].reshape(ALL, FB)
            gram[...] += dot(e, e, ((1,), (1,)))

    gram_of(c)
    pltpu.make_async_remote_copy(
        src_ref=emb.at[pl.ds(0, N_DP // 2)], dst_ref=emb.at[pl.ds(0, N_DP // 2)],
        send_sem=s_send, recv_sem=s_recv, device_id=sibling, device_id_type=MESH,
    ).wait_recv()
    gram_of(1 - c)

    for k in range(1, NX):
        mx(mod(x + k, NX), x).wait_recv()

    inv_temp = it_ref[0]
    info = meta[...].reshape(ALL, 128)
    pos_col, count_col = info[:, 0:1].astype(jnp.int32), info[:, 1:2]
    eye = lax.broadcasted_iota(jnp.int32, (RB, RB), 0) == lax.broadcasted_iota(jnp.int32, (RB, RB), 1)
    blocks = [slice(i * RB, (i + 1) * RB) for i in range(ALL // RB)]

    def as_row(cols):
        return jnp.concatenate(
            [jnp.sum(jnp.where(eye, jnp.broadcast_to(v, (RB, RB)), 0.0), axis=0, keepdims=True) for v in cols],
            axis=1,
        )

    q_cols = []
    for r in blocks:
        norm2 = jnp.sum(jnp.where(eye, gram[r, r], 0.0), axis=1, keepdims=True)
        inv_count = 1.0 / count_col[r]
        q_cols.append(inv_count * lax.rsqrt(norm2 * inv_count * inv_count + 1e-06))
    q_row = as_row(q_cols)
    pos_row = as_row([info[r, 0:1] for r in blocks]).astype(jnp.int32)

    lane_all = lax.broadcasted_iota(jnp.int32, (RB, ALL), 1)
    sub_all = lax.broadcasted_iota(jnp.int32, (RB, ALL), 0)
    lse_cols = []
    loss = jnp.zeros((1, 1), F32)
    for i, r in enumerate(blocks):
        cosine = gram[r, :] * q_cols[i] * q_row
        gram[r, :] = cosine
        logits = jnp.where(lane_all == sub_all + i * RB, -1e30, cosine * inv_temp)
        top = jnp.max(logits, axis=1, keepdims=True)
        sum_exp = jnp.sum(jnp.exp(logits - top), axis=1, keepdims=True)
        lse = top + jnp.log(sum_exp)
        at_pos = jnp.sum(jnp.where(lane_all == pos_col[r], logits, 0.0), axis=1, keepdims=True)
        loss = loss + jnp.sum(lse - at_pos, axis=0, keepdims=True)
        lse_cols.append(lse)
    loss_ref[...] = jnp.broadcast_to(loss * (1.0 / ALL), (1, 128))
    lse_row = as_row(lse_cols)

    for i, r in enumerate(blocks):
        cosine = gram[r, :]
        diagonal = lane_all == sub_all + i * RB
        logits = jnp.where(diagonal, -1e30, cosine * inv_temp)
        own = jnp.exp(logits - lse_cols[i]) - (lane_all == pos_col[r]).astype(F32)
        other = jnp.exp(logits - lse_row) - (sub_all + i * RB == pos_row).astype(F32)
        both = (own + other) * (inv_temp * (1.0 / ALL))
        along = jnp.sum(both * cosine, axis=1, keepdims=True)
        nmat[r, :] = ((both - jnp.where(diagonal, along, 0.0)) * q_cols[i] * q_row).astype(BF16)

    n_all = nmat[...]
    my_rows = pl.ds(pl.multiple_of(dp * DOCS, DOCS), DOCS)

    @pl.loop(0, N_CTX)
    def _(j):
        cols = pl.ds(pl.multiple_of(j * FB, FB), FB)
        e = emb[:, :, cols].reshape(ALL, FB)
        tbuf[...] = dot(n_all, e, ((1,), (0,)))
        gain = gain_ref[:, cols]
        gg_ref[:, cols] = jnp.sum(tbuf[...] * e.astype(F32), axis=0, keepdims=True) / gain
        g16 = tbuf[my_rows, :] * gain
        g_hi = g16.astype(BF16)
        gd_ref[0:DOCS, cols] = g_hi
        gd_ref[DOCS:, cols] = (g16 - g_hi.astype(F32)).astype(BF16)

    oh = jnp.concatenate([onehot, onehot, jnp.zeros((128 - 2 * DOCS, TOK), F32)], axis=0)
    oh_ref[...] = jnp.transpose(oh).astype(BF16)

    def sent(ref, sem):
        pltpu.make_async_remote_copy(
            src_ref=ref, dst_ref=ref, send_sem=sem, recv_sem=s_recv, device_id=sibling, device_id_type=MESH,
        ).wait_send()

    sent(recv.at[pl.ds(0, N_CTX - 1)], p1_send)
    sent(meta_ctx.at[pl.ds(0, N_CTX - 1)], m1_send)
    sent(emb.at[pl.ds(0, NZ - 1), :, pl.ds(0, FB)], z_send)
    sent(meta.at[pl.ds(0, NZ - 1)], mz_send)
    sent(meta.at[pl.ds(0, NZ * (NX - 1))], mx_send)
    sent(emb.at[pl.ds(0, 3)], a_send)
    sent(emb.at[pl.ds(0, 12)], b_send)
    sent(emb.at[pl.ds(0, 16)], s_send)


def final_kernel(h_ref, gd_ref, oh_ref, sc_ref, gg_ref, loss_ref, out_ref, gg_out, loss_out):
    states = h_ref[0]
    gd2 = gd_ref[...]
    select = oh_ref[:, 0:2 * DOCS]
    scale = sc_ref[:, 0:1]
    inner = dot(states, gd2, ((1,), (1,))) * select.astype(F32)
    inner = jnp.sum(inner, axis=1, keepdims=True) * (1.0 / D)
    coef = scale * scale * scale * inner
    for j in range(D // 512):
        cols = slice(j * 512, (j + 1) * 512)
        grad = dot(select, gd2[:, cols], ((1,), (0,)))
        out_ref[0, :, cols] = (scale * grad - states[:, cols].astype(F32) * coef).astype(BF16)
    gg_out[...] = gg_ref[...]
    loss_out[...] = loss_ref[...]


def body(hidden, segments, gain, inv_temp, positives):
    vmem = pl.BlockSpec(memory_space=pltpu.VMEM)
    smem = pl.BlockSpec(memory_space=pltpu.SMEM)
    dma = pltpu.SemaphoreType.DMA
    gd, oh, sc, gg, loss = pl.pallas_call(
        gather_kernel,
        name="pool_gather",
        out_shape=(
            jax.ShapeDtypeStruct((2 * DOCS, D), BF16),
            jax.ShapeDtypeStruct((TOK, 128), BF16),
            jax.ShapeDtypeStruct((TOK, 128), F32),
            jax.ShapeDtypeStruct((1, D), F32),
            jax.ShapeDtypeStruct((1, 128), F32),
        ),
        in_specs=[pl.BlockSpec(memory_space=pl.ANY), vmem, smem, vmem, smem],
        out_specs=(vmem,) * 5,
        scratch_shapes=[
            pltpu.VMEM((TOK, D), BF16),
            pltpu.VMEM((DOCS, D), BF16),
            pltpu.VMEM((N_CTX, DOCS, FB), BF16),
            pltpu.VMEM((N_DP, DOCS, D), BF16),
            pltpu.VMEM((DOCS, 128), F32),
            pltpu.VMEM((N_CTX, DOCS, 128), F32),
            pltpu.VMEM((N_DP, DOCS, 128), F32),
            pltpu.VMEM((ALL, ALL), F32),
            pltpu.VMEM((ALL, ALL), BF16),
            pltpu.VMEM((ALL, FB), F32),
            dma((4,)),
            dma, dma((N_CTX,)), dma, dma((NZ,)), dma, dma((NX,)), dma, dma((N_CTX,)),
            dma, dma((NZ,)), dma, dma((12,)), dma, dma((48,)), dma, dma,
        ],
        compiler_params=pltpu.CompilerParams(collective_id=0, has_side_effects=True),
    )(hidden[0], segments, positives, gain.reshape(1, D), inv_temp.reshape(1))

    rows = 64
    whole = lambda shape: pl.BlockSpec(shape, lambda i: (0, 0))
    grad_hidden, grad_gain, loss = pl.pallas_call(
        final_kernel,
        name="grad_hidden",
        grid=(TOK // rows,),
        out_shape=(
            jax.ShapeDtypeStruct((1, TOK, D), BF16),
            jax.ShapeDtypeStruct((1, D), F32),
            jax.ShapeDtypeStruct((1, 128), F32),
        ),
        in_specs=[
            pl.BlockSpec((1, rows, D), lambda i: (0, i, 0)),
            whole((2 * DOCS, D)),
            pl.BlockSpec((rows, 128), lambda i: (i, 0)),
            pl.BlockSpec((rows, 128), lambda i: (i, 0)),
            whole((1, D)),
            whole((1, 128)),
        ],
        out_specs=(pl.BlockSpec((1, rows, D), lambda i: (0, i, 0)), whole((1, D)), whole((1, 128))),
    )(hidden, gd, oh, sc, gg, loss)
    return grad_hidden, grad_gain.reshape(D), loss[0, 0]


def solution(mesh):
    return jax.shard_map(
        body,
        mesh=mesh,
        in_specs=(P("dp", "ctx", None), P("dp", "ctx"), P(), P(), P(("dp", "ctx"))),
        out_specs=(P("dp", "ctx", None), P(), P()),
        check_vma=False,
    )
```

time: 390 us -> 60.5 us (0.16)
  waiting for transfers between devices: 170 us -> 0 us
  blocking collectives: 169 us -> 0 us
  Pallas kernels: 0 us -> 58.9 us
  matrix products: 16.3 us -> 0 us
  between operations: 16.1 us -> 1.29 us
  other arithmetic: 10 us -> 0 us
  local copies, waits for them, and re-layouts: 8.27 us -> 0 us
    all_gather x1 -> x0, waiting for transfers between devices: 119 us -> none  [body(): emb_all = lax.all_gather(emb_own, ('dp', 'ctx'), axis=0, tiled=True)]
    all_gather x2 -> x0, blocking collectives: 79.8 us -> none  [the longest x1 67 us: body(): grad_rows = lax.all_gather(gmat, ('dp', 'ctx'), axis=0, tiled=True)]
    psum x1 -> x0, blocking collectives: 74 us -> none  [body(): grad_gain, loss = lax.psum((gain_local, loss_local), ('dp', 'ctx'))]
    pallas_call x0 -> x2, Pallas kernels: none -> 58.9 us  [the longest x1 53.5 us: body(): pl.pallas_call(gather_kernel, name='pool_gather', out_shape=(jax.ShapeDty...]
    unnamed x3 -> x0, waiting for transfers between devices: 50.8 us -> none
    dot_general x5 -> x0, matrix products: 16.3 us -> none  [the longest x1 4.75 us: body(): jnp.dot(document_indicator, dsum_seq, precision=lax.Precision.HIGHEST)]
    unnamed x1 -> x0, blocking collectives: 15 us -> none
    unnamed x17 -> x0, local copies, waits for them, and re-layouts: 8.27 us -> none
  transfers between devices with their start and end apart: 2 -> 0, of which waited for: 2 -> 0; matrix products, arithmetic and copies ran while one was open for 0% -> 0% of each run, Pallas kernels for 0% -> 0%
where the time goes in v1:
time: 60.5 us; the launch traced here: 60.1 us
  Pallas kernels  58.9 us (97%)
  between operations  1.29 us (2%)
    pallas_call x1, Pallas kernels, body(): pl.pallas_call(gather_kernel, name='pool_gather', out_shape=(jax.ShapeDty...  53.5 us
    pallas_call x1, Pallas kernels, body(): pl.pallas_call(final_kernel, name='grad_hidden', grid=(TOK // rows,), out...  5.36 us

profile of v1, /device:TPU:1, one launch (start us, length us, event | category | flops | bytes accessed | tf_op | source)
XLA Modules:
  0.0 60.1 jit_solution(11445615925469736014)
XLA Ops:
  1.3 53.5 %pool_gather.1 = (bf16[32,4096]{1,0:T(8,128)(2,1)}, bf16[256,128]{1,0:T(8,128)(2,1)}, f32[256,128]{1,0:T(8,128)}, f32[1,4096]{1,0:T(1,128)}, f32[1,128]{1,0:T(1,128)}) custom-call(bf16[256,4096]{1,0:T(8,128)(2,1)} %bitcast.7, s32[1,256]{1,0:T(1,128)} %seg_ref.1, s32[2]{0:T(128)} %pos_ref.1, f32[1,4096]{1,0:T(1,128)} %bitcast.8, f32[1]{0:T(128)} %bitcast.6.it_ref), custom_call_target="tpu_custom_call" | custom-call | tf_op jit(solution)/shard_map/pool_gather/pallas_call | solution.py:372
  54.8 5.4 %grad_hidden.1 = (bf16[1,256,4096]{2,1,0:T(8,128)(2,1)}, f32[1,4096]{1,0:T(1,128)}, f32[1,128]{1,0:T(1,128)}) custom-call(bf16[1,256,4096]{2,1,0:T(8,128)(2,1)} %h_ref.1, bf16[32,4096]{1,0:T(8,128)(2,1)} %get-tuple-element.11.gd_ref, bf16[256,128]{1,0:T(8,128)(2,1)} %get-tuple-element.12.oh_ref, f32[256,128]{1,0:T(8,128)} %get-tuple-element.13.sc_ref, ...), custom_call_target="tpu_custom_call" | custom-call | tf_op jit(solution)/shard_map/grad_hidden/pallas_call | solution.py:404

commit v2 on v1

--- a/solution.py
+++ b/solution.py
@@ -18,7 +18,6 @@
 TOK = 256
 D = 4096
 FB = D // N_CTX
-PAIR_ORDER = (0, 1, 3, 2)
 RB = 128
 
 
@@ -43,34 +42,37 @@
     a = (1 - c) * x + c * y
     b = (1 - c) * y + c * x
 
-    def at_a(aa):
-        return ((1 - c) * (aa * NZ + z) + c * dp, (1 - c) * ctx + c * (aa * 2 + c))
-
-    def at_b(bb):
-        return ((1 - c) * dp + c * (bb * NZ + z), (1 - c) * (bb * 2 + c) + c * ctx)
-
-    sibling = (dp, ctx + 1 - 2 * c)
-
-    barrier = pltpu.get_barrier_semaphore()
-    peers = [(dp, mod(ctx + k, N_CTX)) for k in range(1, N_CTX)]
-    peers += [(x * NZ + mod(z + k, NZ), ctx) for k in range(1, NZ)]
-    peers += [(mod(x + k, NX) * NZ + z, ctx) for k in range(1, NX)]
-    for peer in peers:
-        pl.semaphore_signal(barrier, inc=1, device_id=peer, device_id_type=MESH)
-
     h_copies = []
     for i in range(4):
         rows = pl.ds(i * (TOK // 4), TOK // 4)
         h_copies.append(pltpu.make_async_copy(h_hbm.at[rows], h.at[rows], h_sem.at[i]))
         h_copies[-1].start()
 
+    def at_a(aa):
+        return ((1 - c) * (aa * NZ + z) + c * dp, (1 - c) * ctx + c * (aa * 2 + c))
+
+    def at_b(bb):
+        return ((1 - c) * dp + c * (bb * NZ + z), (1 - c) * (bb * 2 + c) + c * ctx)
+
+    sibling = (dp, ctx + 1 - 2 * c)
+
+    barrier = pltpu.get_barrier_semaphore()
+    peers = [(x * NZ + mod(z + k, NZ), ctx) for k in (4, 3, 5, 2, 6, 1, 7)]
+    peers += [(dp, mod(ctx + k, N_CTX)) for k in range(1, N_CTX)]
+    peers += [(mod(x + k, NX) * NZ + z, ctx) for k in range(1, NX)]
+    for peer in peers:
+        pl.semaphore_signal(barrier, inc=1, device_id=peer, device_id_type=MESH)
+
     seg = seg_ref[...]
     doc_rows = lax.broadcasted_iota(jnp.int32, (DOCS, TOK), 0)
     onehot = (seg == doc_rows).astype(F32)
-    doc_col = lax.broadcasted_iota(jnp.int32, (DOCS, 128), 0)
     lane = lax.broadcasted_iota(jnp.int32, (DOCS, 128), 1)
-    pos = jnp.where(doc_col == 2 * ctx, pos_ref[0], jnp.where(doc_col == 2 * ctx + 1, pos_ref[1], 0))
-    meta_own[...] = jnp.where(lane == 0, pos.astype(F32), jnp.sum(onehot, axis=1, keepdims=True))
+    counts = jnp.where(
+        lane == DOCS + lax.broadcasted_iota(jnp.int32, (DOCS, 128), 0), jnp.sum(onehot, axis=1, keepdims=True), 0.0
+    )
+    lane1 = lax.broadcasted_iota(jnp.int32, (1, 128), 1)
+    pos = jnp.where(lane1 == 2 * ctx, pos_ref[0], jnp.where(lane1 == 2 * ctx + 1, pos_ref[1], 0))
+    meta_own[...] = pos.astype(F32) + jnp.sum(counts, axis=0, keepdims=True)
 
     squares = []
     for i in range(4):
@@ -87,10 +89,6 @@
     w_hi = weight.astype(BF16)
     w_lo = (weight - w_hi.astype(F32)).astype(BF16)
     w2 = jnp.concatenate([w_hi, w_lo], axis=0)
-    for j in range(N_CTX):
-        cols = slice(j * FB, (j + 1) * FB)
-        both = dot(w2, h[:, cols], ((1,), (0,)))
-        part[:, cols] = ((both[0:DOCS] + both[DOCS:]) * gain_ref[:, cols]).astype(BF16)
 
     pl.semaphore_wait(barrier, len(peers))
 
@@ -106,14 +104,20 @@
             send_sem=m1_send, recv_sem=m1_recv.at[src], device_id=(dp, dst), device_id_type=MESH,
         )
 
+    def partial_sums(j):
+        cols = pl.ds(pl.multiple_of(j * FB, FB), FB)
+        both = dot(w2, h[:, cols], ((1,), (0,)))
+        return (both[0:DOCS] + both[DOCS:]) * gain_ref[:, cols]
+
     others = [mod(ctx + k, N_CTX) for k in (4, 5, 3, 2, 6, 7, 1)]
     for other in others:
+        m1(ctx, other).start()
+    for other in others:
+        part[:, pl.ds(pl.multiple_of(other * FB, FB), FB)] = partial_sums(other).astype(BF16)
         p1(ctx, other).start()
-    for other in others:
-        m1(ctx, other).start()
 
     my_col = pl.ds(pl.multiple_of(ctx * FB, FB), FB)
-    total = part[:, my_col].astype(F32)
+    total = partial_sums(ctx)
     for other in reversed(others):
         p1(other, ctx).wait_recv()
         total = total + recv[other].astype(F32)
@@ -126,9 +130,6 @@
             device_id=(x * NZ + dst, ctx), device_id_type=MESH,
         )
 
-    for k in (4, 3, 5, 2, 6, 1, 7):
-        zcopy(z, mod(z + k, NZ)).start()
-
     def mz(zz, dst):
         ref = meta.at[x * NZ + zz]
         return pltpu.make_async_remote_copy(
@@ -143,112 +144,128 @@
             device_id=(dst * NZ + z, ctx), device_id_type=MESH,
         )
 
+    partner = z + 1 - 2 * mod(z, 2)
+    pair = lax.div(z, 2)
+    pair_at = [2 * mod(pair + k, NZ // 2) for k in (1, 3, 2)]
+    first = [z, partner] + pair_at
+    size = [1, 1, 2, 2, 2]
+    away = [partner] + [pair_at[i] + j for i in (1, 0, 2) for j in range(2)]
+
+    a_off = lambda k: mod(a + k, NX)
+    b_off = lambda k: mod(b + k, NX)
+
+    def block(aa, bb, g):
+        xx = (1 - c) * aa + c * bb
+        yy = (1 - c) * bb + c * aa
+        col = pl.multiple_of((yy * 2 + c) * FB, FB)
+        return emb.at[pl.ds(xx * NZ + first[g], size[g]), :, pl.ds(col, FB)]
+
+    def acopy(am, g, way, to):
+        ref = block(a_off(am), b, g)
+        return pltpu.make_async_remote_copy(
+            src_ref=ref, dst_ref=ref, send_sem=a_send, recv_sem=a_recv.at[3 * g + way],
+            device_id=at_a(to), device_id_type=MESH,
+        )
+
+    def bcopy(am, bm, g, way, to):
+        ref = block(a_off(am), b_off(bm), g)
+        return pltpu.make_async_remote_copy(
+            src_ref=ref, dst_ref=ref, send_sem=b_send, recv_sem=b_recv.at[12 * g + 3 * am + way],
+            device_id=at_b(to), device_id_type=MESH,
+        )
+
+    def sib(am, bm, g):
+        ref = block(a_off(am), b_off(bm), g)
+        pltpu.make_async_remote_copy(
+            src_ref=ref, dst_ref=ref, send_sem=s_send, recv_sem=s_recv,
+            device_id=sibling, device_id_type=MESH,
+        ).start()
+
+    def spread(am, g):
+        bcopy(am, 0, g, 0, b_off(1)).start()
+        bcopy(am, 0, g, 1, b_off(3)).start()
+        sib(am, 0, g)
+
+    def enter(g):
+        for i in range(size[g]):
+            if g > 0:
+                zcopy(first[g] + i, z).wait_recv()
+        for way, k in ((0, 1), (1, 3), (2, 2)):
+            acopy(0, g, way, a_off(k)).start()
+        spread(0, g)
+
+    def along_a(g):
+        for way, k in ((0, 3), (1, 1), (2, 2)):
+            acopy(k, g, way, a).wait_recv()
+            spread(k, g)
+
+    def relay(am, g):
+        bcopy(am, 3, g, 0, b).wait_recv()
+        bcopy(am, 1, g, 1, b).wait_recv()
+        if (g + (am >= 2)) % 2 == 0:
+            bcopy(am, 3, g, 2, b_off(1)).start()
+        else:
+            bcopy(am, 1, g, 2, b_off(3)).start()
+        sib(am, 3, g)
+        sib(am, 1, g)
+
+    def last(am, g):
+        bcopy(am, 2, g, 2, b).wait_recv()
+        sib(am, 2, g)
+
+    for to in away:
+        zcopy(z, to).start()
+    enter(0)
     meta_sum = meta_own[...]
     for other in others:
         m1(other, ctx).wait_recv()
         meta_sum = meta_sum + meta_ctx[other]
     meta[dp] = meta_sum
-    for k in range(1, NZ):
-        mz(z, mod(z + k, NZ)).start()
-
-    a_off = lambda k: mod(a + k, NX)
-    b_off = lambda k: mod(b + k, NX)
-    pair_of = lambda k: mod(lax.div(z, 2) + PAIR_ORDER[k], NZ // 2)
-
-    def block(aa, bb, k):
-        xx = (1 - c) * aa + c * bb
-        yy = (1 - c) * bb + c * aa
-        col = pl.multiple_of((yy * 2 + c) * FB, FB)
-        return emb.at[pl.ds(xx * NZ + 2 * pair_of(k), 2), :, pl.ds(col, FB)]
-
-    def acopy(aa, k, way, to):
-        ref = block(aa, b, k)
-        return pltpu.make_async_remote_copy(
-            src_ref=ref, dst_ref=ref, send_sem=a_send, recv_sem=a_recv.at[3 * k + way],
-            device_id=at_a(to), device_id_type=MESH,
-        )
-
-    def bcopy(am, bb, k, way, to):
-        ref = block(a_off(am), bb, k)
-        return pltpu.make_async_remote_copy(
-            src_ref=ref, dst_ref=ref, send_sem=b_send, recv_sem=b_recv.at[12 * k + 3 * am + way],
-            device_id=at_b(to), device_id_type=MESH,
-        )
-
-    def sib(am, bm, k):
-        ref = block(a_off(am), b_off(bm), k)
-        return pltpu.make_async_remote_copy(
-            src_ref=ref, dst_ref=ref, send_sem=s_send, recv_sem=s_recv,
-            device_id=sibling, device_id_type=MESH,
-        )
-
-    def a_start(k):
-        acopy(a, k, 0, a_off(1)).start()
-        acopy(a, k, 1, a_off(3)).start()
-
-    def b_start(am, k):
-        bcopy(am, b, k, 0, b_off(1)).start()
-        bcopy(am, b, k, 1, b_off(3)).start()
-        sib(am, 0, k).start()
-
-    def a_relay(k):
-        acopy(a_off(3), k, 0, a).wait_recv()
-        acopy(a_off(1), k, 1, a).wait_recv()
-        if k % 2 == 0:
-            acopy(a_off(3), k, 2, a_off(1)).start()
-        else:
-            acopy(a_off(1), k, 2, a_off(3)).start()
-        b_start(3, k)
-        b_start(1, k)
-
-    def a_last(k):
-        acopy(a_off(2), k, 2, a).wait_recv()
-        b_start(2, k)
-
-    def b_relay(am, k):
-        bcopy(am, b_off(3), k, 0, b).wait_recv()
-        bcopy(am, b_off(1), k, 1, b).wait_recv()
-        if (k + (am == 2)) % 2 == 0:
-            bcopy(am, b_off(3), k, 2, b_off(1)).start()
-        else:
-            bcopy(am, b_off(1), k, 2, b_off(3)).start()
-        sib(am, 3, k).start()
-        sib(am, 1, k).start()
-
-    def b_last(am, k):
-        bcopy(am, b_off(2), k, 2, b).wait_recv()
-        sib(am, 2, k).start()
-
-    for t in range(9):
-        if t < 4:
-            for i in range(2):
-                zz = 2 * pair_of(t) + i
-                if t == 0:
-                    zz = z + 1 - 2 * mod(z, 2)
-                    if i == 1:
-                        continue
-                zcopy(zz, z).wait_recv()
-            a_start(t)
-            b_start(0, t)
-        if 1 <= t < 5:
-            a_relay(t - 1)
-            b_relay(0, t - 1)
-        if 2 <= t < 6:
-            a_last(t - 2)
-            b_relay(3, t - 2)
-            b_relay(1, t - 2)
-            b_last(0, t - 2)
-        if 3 <= t < 7:
-            b_relay(2, t - 3)
-            b_last(3, t - 3)
-            b_last(1, t - 3)
-        if 4 <= t < 8:
-            b_last(2, t - 4)
-        if t == 3:
-            for k in range(1, NZ):
-                mz(mod(z + k, NZ), z).wait_recv()
-            for k in range(1, NX):
-                mx(x, mod(x + k, NX)).start()
+    for to in away:
+        mz(z, to).start()
+
+    enter(1)
+    along_a(0)
+    enter(2)
+    relay(0, 0)
+    enter(3)
+    along_a(1)
+    relay(0, 1)
+    enter(4)
+    for am in (3, 1, 2):
+        relay(am, 0)
+    along_a(2)
+    last(0, 0)
+    for am in (3, 1, 2):
+        relay(am, 1)
+    relay(0, 2)
+    along_a(3)
+    for to in away:
+        mz(to, z).wait_recv()
+    for k in range(1, NX):
+        mx(x, mod(x + k, NX)).start()
+    for am in (3, 1, 2):
+        last(am, 0)
+    last(0, 1)
+    relay(0, 3)
+    along_a(4)
+    for am in (3, 1, 2):
+        relay(am, 2)
+    relay(0, 4)
+    for am in (3, 1, 2):
+        last(am, 1)
+    last(0, 2)
+    for am in (3, 1, 2):
+        relay(am, 3)
+    last(0, 3)
+    for am in (3, 1, 2):
+        relay(am, 4)
+    for am in (3, 1, 2):
+        last(am, 2)
+    for g in (3, 4):
+        for am in (0, 3, 1, 2):
+            if (am, g) != (0, 3):
+                last(am, g)
 
     gram[...] = jnp.zeros_like(gram)
 
@@ -270,8 +287,11 @@
         mx(mod(x + k, NX), x).wait_recv()
 
     inv_temp = it_ref[0]
-    info = meta[...].reshape(ALL, 128)
-    pos_col, count_col = info[:, 0:1].astype(jnp.int32), info[:, 1:2]
+    info = jnp.broadcast_to(meta[...], (N_DP, DOCS, 128)).reshape(ALL, 128)
+    at = lax.broadcasted_iota(jnp.int32, (ALL, 128), 1) - mod(lax.broadcasted_iota(jnp.int32, (ALL, 128), 0), DOCS)
+    pos_f = jnp.sum(jnp.where(at == 0, info, 0.0), axis=1, keepdims=True)
+    pos_col = pos_f.astype(jnp.int32)
+    count_col = jnp.sum(jnp.where(at == DOCS, info, 0.0), axis=1, keepdims=True)
     eye = lax.broadcasted_iota(jnp.int32, (RB, RB), 0) == lax.broadcasted_iota(jnp.int32, (RB, RB), 1)
     blocks = [slice(i * RB, (i + 1) * RB) for i in range(ALL // RB)]
 
@@ -287,7 +307,7 @@
         inv_count = 1.0 / count_col[r]
         q_cols.append(inv_count * lax.rsqrt(norm2 * inv_count * inv_count + 1e-06))
     q_row = as_row(q_cols)
-    pos_row = as_row([info[r, 0:1] for r in blocks]).astype(jnp.int32)
+    pos_row = as_row([pos_f[r] for r in blocks]).astype(jnp.int32)
 
     lane_all = lax.broadcasted_iota(jnp.int32, (RB, ALL), 1)
     sub_all = lax.broadcasted_iota(jnp.int32, (RB, ALL), 0)
@@ -349,18 +369,22 @@
     sent(emb.at[pl.ds(0, 16)], s_send)
 
 
-def final_kernel(h_ref, gd_ref, oh_ref, sc_ref, gg_ref, loss_ref, out_ref, gg_out, loss_out):
-    states = h_ref[0]
-    gd2 = gd_ref[...]
+def final_kernel(h_ref, gd_ref, oh_ref, sc_ref, gg_ref, loss_ref, out_ref, gg_out, loss_out, grad):
     select = oh_ref[:, 0:2 * DOCS]
     scale = sc_ref[:, 0:1]
-    inner = dot(states, gd2, ((1,), (1,))) * select.astype(F32)
-    inner = jnp.sum(inner, axis=1, keepdims=True) * (1.0 / D)
+    acc = jnp.zeros((select.shape[0], 128), F32)
+    for j in range(D // 512):
+        cols = slice(j * 512, (j + 1) * 512)
+        part = dot(select, gd_ref[:, cols], ((1,), (0,)))
+        grad[:, cols] = part
+        prod = part * h_ref[0, :, cols].astype(F32)
+        for k in range(4):
+            acc = acc + prod[:, k * 128:(k + 1) * 128]
+    inner = jnp.sum(acc, axis=1, keepdims=True) * (1.0 / D)
     coef = scale * scale * scale * inner
     for j in range(D // 512):
         cols = slice(j * 512, (j + 1) * 512)
-        grad = dot(select, gd2[:, cols], ((1,), (0,)))
-        out_ref[0, :, cols] = (scale * grad - states[:, cols].astype(F32) * coef).astype(BF16)
+        out_ref[0, :, cols] = (scale * grad[:, cols] - h_ref[0, :, cols].astype(F32) * coef).astype(BF16)
     gg_out[...] = gg_ref[...]
     loss_out[...] = loss_ref[...]
 
@@ -386,15 +410,15 @@
             pltpu.VMEM((DOCS, D), BF16),
             pltpu.VMEM((N_CTX, DOCS, FB), BF16),
             pltpu.VMEM((N_DP, DOCS, D), BF16),
-            pltpu.VMEM((DOCS, 128), F32),
-            pltpu.VMEM((N_CTX, DOCS, 128), F32),
-            pltpu.VMEM((N_DP, DOCS, 128), F32),
+            pltpu.VMEM((1, 128), F32),
+            pltpu.VMEM((N_CTX, 1, 128), F32),
+            pltpu.VMEM((N_DP, 1, 128), F32),
             pltpu.VMEM((ALL, ALL), F32),
             pltpu.VMEM((ALL, ALL), BF16),
             pltpu.VMEM((ALL, FB), F32),
             dma((4,)),
             dma, dma((N_CTX,)), dma, dma((NZ,)), dma, dma((NX,)), dma, dma((N_CTX,)),
-            dma, dma((NZ,)), dma, dma((12,)), dma, dma((48,)), dma, dma,
+            dma, dma((NZ,)), dma, dma((15,)), dma, dma((60,)), dma, dma,
         ],
         compiler_params=pltpu.CompilerParams(collective_id=0, has_side_effects=True),
     )(hidden[0], segments, positives, gain.reshape(1, D), inv_temp.reshape(1))
@@ -419,6 +443,7 @@
             whole((1, 128)),
         ],
         out_specs=(pl.BlockSpec((1, rows, D), lambda i: (0, i, 0)), whole((1, D)), whole((1, 128))),
+        scratch_shapes=[pltpu.VMEM((rows, D), F32)],
     )(hidden, gd, oh, sc, gg, loss)
     return grad_hidden, grad_gain.reshape(D), loss[0, 0]
 

time: 60.5 us -> 51.6 us (0.85)
  Pallas kernels: 58.9 us -> 50.1 us
    pallas_call x1, Pallas kernels: 53.5 us -> 45.1 us  [body(): pl.pallas_call(gather_kernel, name='pool_gather', out_shape=(jax.ShapeDty...]
where the time goes in v2:
time: 51.6 us; the launch traced here: 51.4 us
  Pallas kernels  50.1 us (97%)
  between operations  1.29 us (2%)
    pallas_call x1, Pallas kernels, body(): pl.pallas_call(gather_kernel, name='pool_gather', out_shape=(jax.ShapeDty...  45.1 us
    pallas_call x1, Pallas kernels, body(): pl.pallas_call(final_kernel, name='grad_hidden', grid=(TOK // rows,), out...  5 us

profile of v2, /device:TPU:1, one launch (start us, length us, event | category | flops | bytes accessed | tf_op | source)
XLA Modules:
  0.0 51.4 jit_solution(15701730197868346857)
XLA Ops:
  1.3 45.1 %pool_gather.1 = (bf16[32,4096]{1,0:T(8,128)(2,1)}, bf16[256,128]{1,0:T(8,128)(2,1)}, f32[256,128]{1,0:T(8,128)}, f32[1,4096]{1,0:T(1,128)}, f32[1,128]{1,0:T(1,128)}) custom-call(bf16[256,4096]{1,0:T(8,128)(2,1)} %bitcast.7, s32[1,256]{1,0:T(1,128)} %seg_ref.1, s32[2]{0:T(128)} %pos_ref.1, f32[1,4096]{1,0:T(1,128)} %bitcast.8, f32[1]{0:T(128)} %bitcast.6.it_ref), custom_call_target="tpu_custom_call" | custom-call | tf_op jit(solution)/shard_map/pool_gather/pallas_call | solution.py:396
  46.4 5.0 %grad_hidden.1 = (bf16[1,256,4096]{2,1,0:T(8,128)(2,1)}, f32[1,4096]{1,0:T(1,128)}, f32[1,128]{1,0:T(1,128)}) custom-call(bf16[1,256,4096]{2,1,0:T(8,128)(2,1)} %h_ref.1, bf16[32,4096]{1,0:T(8,128)(2,1)} %get-tuple-element.11.gd_ref, bf16[256,128]{1,0:T(8,128)(2,1)} %get-tuple-element.12.oh_ref, f32[256,128]{1,0:T(8,128)} %get-tuple-element.13.sc_ref, ...), custom_call_target="tpu_custom_call" | custom-call | tf_op jit(solution)/shard_map/grad_hidden/pallas_call | solution.py:428

commit v3 on v2

--- a/solution.py
+++ b/solution.py
@@ -18,6 +18,8 @@
 TOK = 256
 D = 4096
 FB = D // N_CTX
+HALF = ALL // 2
+ROWS = 32
 RB = 128
 
 
@@ -30,10 +32,10 @@
 
 
 def gather_kernel(
-    h_hbm, seg_ref, pos_ref, gain_ref, it_ref,
-    gd_ref, oh_ref, sc_ref, gg_ref, loss_ref,
-    h, part, recv, emb, meta_own, meta_ctx, meta, gram, nmat, tbuf,
-    h_sem, m1_send, m1_recv, mz_send, mz_recv, mx_send, mx_recv, p1_send, p1_recv,
+    h_hbm, seg_hbm, pos_ref, gain_hbm, it_ref,
+    gd_ref, oh_ref, sc_ref, gg_ref, loss_ref, h,
+    seg_ref, gain_ref, part, recv, emb, meta_own, meta_ctx, meta, gram, nmat,
+    in_sem, h_sem, m1_send, m1_recv, mz_send, mz_recv, mx_send, mx_recv, p1_send, p1_recv,
     z_send, z_recv, a_send, a_recv, b_send, b_recv, s_send, s_recv,
 ):
     dp, ctx = lax.axis_index("dp"), lax.axis_index("ctx")
@@ -42,11 +44,15 @@
     a = (1 - c) * x + c * y
     b = (1 - c) * y + c * x
 
+    seg_copy = pltpu.make_async_copy(seg_hbm, seg_ref, in_sem.at[0])
+    seg_copy.start()
     h_copies = []
     for i in range(4):
         rows = pl.ds(i * (TOK // 4), TOK // 4)
         h_copies.append(pltpu.make_async_copy(h_hbm.at[rows], h.at[rows], h_sem.at[i]))
         h_copies[-1].start()
+    gain_copy = pltpu.make_async_copy(gain_hbm, gain_ref, in_sem.at[1])
+    gain_copy.start()
 
     def at_a(aa):
         return ((1 - c) * (aa * NZ + z) + c * dp, (1 - c) * ctx + c * (aa * 2 + c))
@@ -57,12 +63,13 @@
     sibling = (dp, ctx + 1 - 2 * c)
 
     barrier = pltpu.get_barrier_semaphore()
-    peers = [(x * NZ + mod(z + k, NZ), ctx) for k in (4, 3, 5, 2, 6, 1, 7)]
+    peers = [(x * NZ + mod(z + k, NZ), ctx) for k in (2, 6, 1, 7)]
     peers += [(dp, mod(ctx + k, N_CTX)) for k in range(1, N_CTX)]
     peers += [(mod(x + k, NX) * NZ + z, ctx) for k in range(1, NX)]
     for peer in peers:
         pl.semaphore_signal(barrier, inc=1, device_id=peer, device_id_type=MESH)
 
+    seg_copy.wait()
     seg = seg_ref[...]
     doc_rows = lax.broadcasted_iota(jnp.int32, (DOCS, TOK), 0)
     onehot = (seg == doc_rows).astype(F32)
@@ -89,8 +96,7 @@
     w_hi = weight.astype(BF16)
     w_lo = (weight - w_hi.astype(F32)).astype(BF16)
     w2 = jnp.concatenate([w_hi, w_lo], axis=0)
-
-    pl.semaphore_wait(barrier, len(peers))
+    gain_copy.wait()
 
     def p1(src, dst):
         return pltpu.make_async_remote_copy(
@@ -104,20 +110,20 @@
             send_sem=m1_send, recv_sem=m1_recv.at[src], device_id=(dp, dst), device_id_type=MESH,
         )
 
-    def partial_sums(j):
-        cols = pl.ds(pl.multiple_of(j * FB, FB), FB)
+    for j in range(N_CTX):
+        cols = slice(j * FB, (j + 1) * FB)
         both = dot(w2, h[:, cols], ((1,), (0,)))
-        return (both[0:DOCS] + both[DOCS:]) * gain_ref[:, cols]
-
+        part[:, cols] = ((both[0:DOCS] + both[DOCS:]) * gain_ref[:, cols]).astype(BF16)
+
+    pl.semaphore_wait(barrier, len(peers))
     others = [mod(ctx + k, N_CTX) for k in (4, 5, 3, 2, 6, 7, 1)]
     for other in others:
+        p1(ctx, other).start()
+    for other in others:
         m1(ctx, other).start()
-    for other in others:
-        part[:, pl.ds(pl.multiple_of(other * FB, FB), FB)] = partial_sums(other).astype(BF16)
-        p1(ctx, other).start()
 
     my_col = pl.ds(pl.multiple_of(ctx * FB, FB), FB)
-    total = partial_sums(ctx)
+    total = part[:, my_col].astype(F32)
     for other in reversed(others):
         p1(other, ctx).wait_recv()
         total = total + recv[other].astype(F32)
@@ -144,12 +150,30 @@
             device_id=(dst * NZ + z, ctx), device_id_type=MESH,
         )
 
-    partner = z + 1 - 2 * mod(z, 2)
-    pair = lax.div(z, 2)
-    pair_at = [2 * mod(pair + k, NZ // 2) for k in (1, 3, 2)]
-    first = [z, partner] + pair_at
+    odd = mod(z, 2)
+    z_off = lambda k: mod(z + k + NZ, NZ)
+    pair_off = lambda k: 2 * mod(lax.div(z, 2) + k, NZ // 2)
+    first = [z, z + 1 - 2 * odd, pair_off(3 - 2 * odd), pair_off(1 + 2 * odd), pair_off(2)]
     size = [1, 1, 2, 2, 2]
-    away = [partner] + [pair_at[i] + j for i in (1, 0, 2) for j in range(2)]
+
+    def z_own(copy):
+        for k in (1, -1, 2, -2):
+            copy(z, z_off(k)).start()
+
+    def z_near(copy):
+        for k in (1, -1):
+            copy(z_off(k), z).wait_recv()
+            copy(z_off(k), z_off(-2 * k)).start()
+
+    def z_next(copy):
+        way = 2 - 4 * odd
+        for k in (2, -2):
+            copy(z_off(k), z).wait_recv()
+        copy(z_off(way), z_off(-way)).start()
+
+    def z_far(copy, ks):
+        for k in ks:
+            copy(z_off(k), z).wait_recv()
 
     a_off = lambda k: mod(a + k, NX)
     b_off = lambda k: mod(b + k, NX)
@@ -187,9 +211,6 @@
         sib(am, 0, g)
 
     def enter(g):
-        for i in range(size[g]):
-            if g > 0:
-                zcopy(first[g] + i, z).wait_recv()
         for way, k in ((0, 1), (1, 3), (2, 2)):
             acopy(0, g, way, a_off(k)).start()
         spread(0, g)
@@ -213,42 +234,45 @@
         bcopy(am, 2, g, 2, b).wait_recv()
         sib(am, 2, g)
 
-    for to in away:
-        zcopy(z, to).start()
+    z_own(zcopy)
     enter(0)
     meta_sum = meta_own[...]
     for other in others:
         m1(other, ctx).wait_recv()
         meta_sum = meta_sum + meta_ctx[other]
     meta[dp] = meta_sum
-    for to in away:
-        mz(z, to).start()
-
+    z_own(mz)
+
+    z_near(zcopy)
     enter(1)
     along_a(0)
+    z_next(zcopy)
     enter(2)
     relay(0, 0)
+    along_a(1)
+    z_far(zcopy, (3, -3))
     enter(3)
-    along_a(1)
     relay(0, 1)
+    z_near(mz)
+    along_a(2)
+    z_far(zcopy, (4,))
     enter(4)
+    z_next(mz)
     for am in (3, 1, 2):
         relay(am, 0)
-    along_a(2)
     last(0, 0)
+    along_a(3)
     for am in (3, 1, 2):
         relay(am, 1)
     relay(0, 2)
-    along_a(3)
-    for to in away:
-        mz(to, z).wait_recv()
+    z_far(mz, (3, -3, 4))
     for k in range(1, NX):
         mx(x, mod(x + k, NX)).start()
+    along_a(4)
     for am in (3, 1, 2):
         last(am, 0)
     last(0, 1)
     relay(0, 3)
-    along_a(4)
     for am in (3, 1, 2):
         relay(am, 2)
     relay(0, 4)
@@ -330,23 +354,30 @@
         cosine = gram[r, :]
         diagonal = lane_all == sub_all + i * RB
         logits = jnp.where(diagonal, -1e30, cosine * inv_temp)
-        own = jnp.exp(logits - lse_cols[i]) - (lane_all == pos_col[r]).astype(F32)
-        other = jnp.exp(logits - lse_row) - (sub_all + i * RB == pos_row).astype(F32)
-        both = (own + other) * (inv_temp * (1.0 / ALL))
+        factor = inv_temp * (1.0 / ALL)
+        own = (jnp.exp(logits - lse_cols[i]) - (lane_all == pos_col[r]).astype(F32)) * factor
+        other = (jnp.exp(logits - lse_row) - (sub_all + i * RB == pos_row).astype(F32)) * factor
+        both = own.astype(BF16).astype(F32) + other.astype(BF16).astype(F32)
         along = jnp.sum(both * cosine, axis=1, keepdims=True)
-        nmat[r, :] = ((both - jnp.where(diagonal, along, 0.0)) * q_cols[i] * q_row).astype(BF16)
-
-    n_all = nmat[...]
-    my_rows = pl.ds(pl.multiple_of(dp * DOCS, DOCS), DOCS)
-
-    @pl.loop(0, N_CTX)
-    def _(j):
-        cols = pl.ds(pl.multiple_of(j * FB, FB), FB)
+        grads = (both - jnp.where(diagonal, along, 0.0)) * q_cols[i] * q_row
+        gram[r, :] = grads
+        if i < 2:
+            grads = jnp.where(lane_all < HALF, grads, 2.0 * grads)
+        nmat[r, :] = grads.astype(BF16)
+
+    n_own = gram[pl.ds(pl.multiple_of(dp * DOCS, DOCS), DOCS), :]
+    n_hi = n_own.astype(BF16)
+    n_own = jnp.concatenate([n_hi, (n_own - n_hi.astype(F32)).astype(BF16)], axis=0)
+    n_top, n_low = nmat[0:HALF, :], nmat[HALF:, HALF:]
+    for j in range(N_CTX):
+        cols = slice(j * FB, (j + 1) * FB)
         e = emb[:, :, cols].reshape(ALL, FB)
-        tbuf[...] = dot(n_all, e, ((1,), (0,)))
+        top = dot(n_top, e, ((1,), (0,))) * e[0:HALF].astype(F32)
+        low = dot(n_low, e[HALF:], ((1,), (0,))) * e[HALF:].astype(F32)
         gain = gain_ref[:, cols]
-        gg_ref[:, cols] = jnp.sum(tbuf[...] * e.astype(F32), axis=0, keepdims=True) / gain
-        g16 = tbuf[my_rows, :] * gain
+        gg_ref[:, cols] = (jnp.sum(top, axis=0, keepdims=True) + jnp.sum(low, axis=0, keepdims=True)) / gain
+        both = dot(n_own, e, ((1,), (0,)))
+        g16 = (both[0:DOCS] + both[DOCS:]) * gain
         g_hi = g16.astype(BF16)
         gd_ref[0:DOCS, cols] = g_hi
         gd_ref[DOCS:, cols] = (g16 - g_hi.astype(F32)).astype(BF16)
@@ -369,31 +400,39 @@
     sent(emb.at[pl.ds(0, 16)], s_send)
 
 
-def final_kernel(h_ref, gd_ref, oh_ref, sc_ref, gg_ref, loss_ref, out_ref, gg_out, loss_out, grad):
+def final_kernel(h_ref, gd_ref, oh_ref, sc_ref, gg_ref, loss_ref, out_hbm, gg_out, loss_out, grad, out, sem):
     select = oh_ref[:, 0:2 * DOCS]
-    scale = sc_ref[:, 0:1]
-    acc = jnp.zeros((select.shape[0], 128), F32)
-    for j in range(D // 512):
-        cols = slice(j * 512, (j + 1) * 512)
-        part = dot(select, gd_ref[:, cols], ((1,), (0,)))
-        grad[:, cols] = part
-        prod = part * h_ref[0, :, cols].astype(F32)
-        for k in range(4):
-            acc = acc + prod[:, k * 128:(k + 1) * 128]
-    inner = jnp.sum(acc, axis=1, keepdims=True) * (1.0 / D)
-    coef = scale * scale * scale * inner
-    for j in range(D // 512):
-        cols = slice(j * 512, (j + 1) * 512)
-        out_ref[0, :, cols] = (scale * grad[:, cols] - h_ref[0, :, cols].astype(F32) * coef).astype(BF16)
+    for j in range(D // FB):
+        cols = slice(j * FB, (j + 1) * FB)
+        grad[:, cols] = dot(select, gd_ref[:, cols], ((1,), (0,)))
+    copies = []
+    for i in range(TOK // ROWS):
+        r = slice(i * ROWS, (i + 1) * ROWS)
+        acc = jnp.zeros((ROWS, 128), F32)
+        for j in range(D // 128):
+            cols = slice(j * 128, (j + 1) * 128)
+            acc = acc + grad[r, cols] * h_ref[r, cols].astype(F32)
+        inner = jnp.sum(acc, axis=1, keepdims=True) * (1.0 / D)
+        scale = sc_ref[r, 0:1]
+        coef = scale * scale * scale * inner
+        for j in range(D // 512):
+            cols = slice(j * 512, (j + 1) * 512)
+            out[r, cols] = (scale * grad[r, cols] - h_ref[r, cols].astype(F32) * coef).astype(BF16)
+        copies.append(pltpu.make_async_copy(out.at[pl.ds(i * ROWS, ROWS)], out_hbm.at[0, pl.ds(i * ROWS, ROWS)], sem.at[i]))
+        copies[-1].start()
     gg_out[...] = gg_ref[...]
     loss_out[...] = loss_ref[...]
+    for copy in copies:
+        copy.wait()
 
 
 def body(hidden, segments, gain, inv_temp, positives):
+    hbm = lambda v: pltpu.with_memory_space_constraint(v, pltpu.HBM)
     vmem = pl.BlockSpec(memory_space=pltpu.VMEM)
+    in_hbm = pl.BlockSpec(memory_space=pltpu.HBM)
     smem = pl.BlockSpec(memory_space=pltpu.SMEM)
     dma = pltpu.SemaphoreType.DMA
-    gd, oh, sc, gg, loss = pl.pallas_call(
+    gd, oh, sc, gg, loss, h = pl.pallas_call(
         gather_kernel,
         name="pool_gather",
         out_shape=(
@@ -402,11 +441,13 @@
             jax.ShapeDtypeStruct((TOK, 128), F32),
             jax.ShapeDtypeStruct((1, D), F32),
             jax.ShapeDtypeStruct((1, 128), F32),
+            jax.ShapeDtypeStruct((TOK, D), BF16),
         ),
-        in_specs=[pl.BlockSpec(memory_space=pl.ANY), vmem, smem, vmem, smem],
-        out_specs=(vmem,) * 5,
+        in_specs=[in_hbm, in_hbm, smem, in_hbm, smem],
+        out_specs=(vmem,) * 6,
         scratch_shapes=[
-            pltpu.VMEM((TOK, D), BF16),
+            pltpu.VMEM((1, TOK), jnp.int32),
+            pltpu.VMEM((1, D), F32),
             pltpu.VMEM((DOCS, D), BF16),
             pltpu.VMEM((N_CTX, DOCS, FB), BF16),
             pltpu.VMEM((N_DP, DOCS, D), BF16),
@@ -415,36 +456,27 @@
             pltpu.VMEM((N_DP, 1, 128), F32),
             pltpu.VMEM((ALL, ALL), F32),
             pltpu.VMEM((ALL, ALL), BF16),
-            pltpu.VMEM((ALL, FB), F32),
+            dma((2,)),
             dma((4,)),
             dma, dma((N_CTX,)), dma, dma((NZ,)), dma, dma((NX,)), dma, dma((N_CTX,)),
             dma, dma((NZ,)), dma, dma((15,)), dma, dma((60,)), dma, dma,
         ],
-        compiler_params=pltpu.CompilerParams(collective_id=0, has_side_effects=True),
-    )(hidden[0], segments, positives, gain.reshape(1, D), inv_temp.reshape(1))
-
-    rows = 64
-    whole = lambda shape: pl.BlockSpec(shape, lambda i: (0, 0))
+        compiler_params=pltpu.CompilerParams(collective_id=0, has_side_effects=True, vmem_limit_bytes=20 << 20),
+    )(hbm(hidden[0]), hbm(segments), hbm(positives), hbm(gain.reshape(1, D)), inv_temp.reshape(1))
+
     grad_hidden, grad_gain, loss = pl.pallas_call(
         final_kernel,
         name="grad_hidden",
-        grid=(TOK // rows,),
         out_shape=(
             jax.ShapeDtypeStruct((1, TOK, D), BF16),
             jax.ShapeDtypeStruct((1, D), F32),
             jax.ShapeDtypeStruct((1, 128), F32),
         ),
-        in_specs=[
-            pl.BlockSpec((1, rows, D), lambda i: (0, i, 0)),
-            whole((2 * DOCS, D)),
-            pl.BlockSpec((rows, 128), lambda i: (i, 0)),
-            pl.BlockSpec((rows, 128), lambda i: (i, 0)),
-            whole((1, D)),
-            whole((1, 128)),
-        ],
-        out_specs=(pl.BlockSpec((1, rows, D), lambda i: (0, i, 0)), whole((1, D)), whole((1, 128))),
-        scratch_shapes=[pltpu.VMEM((rows, D), F32)],
-    )(hidden, gd, oh, sc, gg, loss)
+        in_specs=[vmem] * 6,
+        out_specs=(pl.BlockSpec(memory_space=pltpu.HBM), vmem, vmem),
+        scratch_shapes=[pltpu.VMEM((TOK, D), F32), pltpu.VMEM((TOK, D), BF16), dma((TOK // ROWS,))],
+        compiler_params=pltpu.CompilerParams(vmem_limit_bytes=20 << 20),
+    )(h, gd, oh, sc, gg, loss)
     return grad_hidden, grad_gain.reshape(D), loss[0, 0]
 
 

time: 51.6 us -> 48 us (0.930)
  Pallas kernels: 50.1 us -> 46.6 us
    pallas_call x1, Pallas kernels: 5 us -> 2.95 us  [body(): pl.pallas_call(final_kernel, name='grad_hidden', out_shape=(jax.ShapeDtyp...]
    pallas_call x1, Pallas kernels: 45.1 us -> 43.6 us  [body(): pl.pallas_call(gather_kernel, name='pool_gather', out_shape=(jax.ShapeDty...]
where the time goes in v3:
time: 48 us; the launch traced here: 47.9 us
  Pallas kernels  46.6 us (97%)
  between operations  1.29 us (3%)
    pallas_call x1, Pallas kernels, body(): pl.pallas_call(gather_kernel, name='pool_gather', out_shape=(jax.ShapeDty...  43.6 us
    pallas_call x1, Pallas kernels, body(): pl.pallas_call(final_kernel, name='grad_hidden', out_shape=(jax.ShapeDtyp...  2.95 us

profile of v3, /device:TPU:1, one launch (start us, length us, event | category | flops | bytes accessed | tf_op | source)
XLA Modules:
  0.0 47.9 jit_solution(3085517413959592752)
XLA Ops:
  1.3 43.6 %pool_gather.1 = (bf16[32,4096]{1,0:T(8,128)(2,1)S(1)}, bf16[256,128]{1,0:T(8,128)(2,1)S(1)}, f32[256,128]{1,0:T(8,128)S(1)}, f32[1,4096]{1,0:T(1,128)S(1)}, f32...) custom-call(bf16[256,4096]{1,0:T(8,128)(2,1)} %bitcast.7, s32[1,256]{1,0:T(1,128)} %seg_hbm.1, s32[2]{0:T(128)} %pos_ref.1, ...), custom_call_target="tpu_custom_call" | custom-call | tf_op jit(solution)/shard_map/pool_gather/pallas_call | solution.py:435
  44.9 2.9 %grad_hidden.1 = (bf16[1,256,4096]{2,1,0:T(8,128)(2,1)}, f32[1,4096]{1,0:T(1,128)}, f32[1,128]{1,0:T(1,128)}) custom-call(bf16[256,4096]{1,0:T(8,128)(2,1)S(1)} %get-tuple-element.12.h_ref, bf16[32,4096]{1,0:T(8,128)(2,1)S(1)} %get-tuple-element.13.gd_ref, bf16[256,128]{1,0:T(8,128)(2,1)S(1)} %get-tuple-element.14.oh_ref, ...), custom_call_target="tpu_custom_call" | custom-call | tf_op jit(solution)/shard_map/grad_hidden/pallas_call | solution.py:467

commit v4 on v3

--- a/solution.py
+++ b/solution.py
@@ -20,6 +20,7 @@
 FB = D // N_CTX
 HALF = ALL // 2
 ROWS = 32
+DIRECT = (3, 4)
 RB = 128
 
 
@@ -208,6 +209,8 @@
     def spread(am, g):
         bcopy(am, 0, g, 0, b_off(1)).start()
         bcopy(am, 0, g, 1, b_off(3)).start()
+        if g in DIRECT:
+            bcopy(am, 0, g, 2, b_off(2)).start()
         sib(am, 0, g)
 
     def enter(g):
@@ -223,7 +226,9 @@
     def relay(am, g):
         bcopy(am, 3, g, 0, b).wait_recv()
         bcopy(am, 1, g, 1, b).wait_recv()
-        if (g + (am >= 2)) % 2 == 0:
+        if g in DIRECT:
+            pass
+        elif (g + (am >= 2)) % 2 == 0:
             bcopy(am, 3, g, 2, b_off(1)).start()
         else:
             bcopy(am, 1, g, 2, b_off(3)).start()
@@ -242,70 +247,85 @@
         meta_sum = meta_sum + meta_ctx[other]
     meta[dp] = meta_sum
     z_own(mz)
-
     z_near(zcopy)
     enter(1)
+    z_near(mz)
     along_a(0)
+    relay(0, 0)
     z_next(zcopy)
     enter(2)
-    relay(0, 0)
+    z_next(mz)
     along_a(1)
     z_far(zcopy, (3, -3))
     enter(3)
     relay(0, 1)
-    z_near(mz)
     along_a(2)
     z_far(zcopy, (4,))
     enter(4)
-    z_next(mz)
-    for am in (3, 1, 2):
-        relay(am, 0)
-    last(0, 0)
-    along_a(3)
-    for am in (3, 1, 2):
-        relay(am, 1)
-    relay(0, 2)
     z_far(mz, (3, -3, 4))
     for k in range(1, NX):
         mx(x, mod(x + k, NX)).start()
+    relay(3, 0)
+    relay(1, 0)
+    relay(2, 0)
+    along_a(3)
+    relay(0, 2)
+    last(0, 0)
     along_a(4)
-    for am in (3, 1, 2):
-        last(am, 0)
+    relay(3, 1)
+    relay(1, 1)
+    relay(2, 1)
+    last(3, 0)
+    last(1, 0)
+    last(2, 0)
+    relay(0, 3)
     last(0, 1)
-    relay(0, 3)
-    for am in (3, 1, 2):
-        relay(am, 2)
+    relay(3, 2)
+    relay(1, 2)
+    relay(2, 2)
     relay(0, 4)
-    for am in (3, 1, 2):
-        last(am, 1)
+    last(3, 1)
+    last(1, 1)
+    last(2, 1)
     last(0, 2)
-    for am in (3, 1, 2):
-        relay(am, 3)
+    relay(3, 3)
+    relay(1, 3)
+    relay(2, 3)
+    relay(3, 4)
+    relay(1, 4)
+    relay(2, 4)
+    last(3, 2)
+    last(1, 2)
+    last(2, 2)
     last(0, 3)
-    for am in (3, 1, 2):
-        relay(am, 4)
-    for am in (3, 1, 2):
-        last(am, 2)
-    for g in (3, 4):
-        for am in (0, 3, 1, 2):
-            if (am, g) != (0, 3):
-                last(am, g)
-
-    gram[...] = jnp.zeros_like(gram)
-
-    def gram_of(core):
-        @pl.loop(0, NY)
-        def _(yy):
+    last(3, 3)
+    last(1, 3)
+    last(2, 3)
+    last(0, 4)
+    last(3, 4)
+    last(1, 4)
+    last(2, 4)
+
+    def gram_of(core, first_time):
+        for yy in range(NY):
             col = pl.multiple_of((yy * 2 + core) * FB, FB)
             e = emb[:, :, pl.ds(col, FB)].reshape(ALL, FB)
-            gram[...] += dot(e, e, ((1,), (1,)))
-
-    gram_of(c)
+            top = dot(e[0:HALF], e, ((1,), (1,)))
+            low = dot(e[HALF:], e[HALF:], ((1,), (1,)))
+            if first_time and yy == 0:
+                gram[0:HALF, :] = top
+                gram[HALF:, HALF:] = low
+            else:
+                gram[0:HALF, :] += top
+                gram[HALF:, HALF:] += low
+
+    gram_of(c, True)
     pltpu.make_async_remote_copy(
         src_ref=emb.at[pl.ds(0, N_DP // 2)], dst_ref=emb.at[pl.ds(0, N_DP // 2)],
         send_sem=s_send, recv_sem=s_recv, device_id=sibling, device_id_type=MESH,
     ).wait_recv()
-    gram_of(1 - c)
+    gram_of(1 - c, False)
+    gram[HALF:, 0:HALF] = jnp.transpose(gram[0:HALF, HALF:])
 
     for k in range(1, NX):
         mx(mod(x + k, NX), x).wait_recv()
@@ -338,9 +358,11 @@
     lse_cols = []
     loss = jnp.zeros((1, 1), F32)
     for i, r in enumerate(blocks):
-        cosine = gram[r, :] * q_cols[i] * q_row
-        gram[r, :] = cosine
-        logits = jnp.where(lane_all == sub_all + i * RB, -1e30, cosine * inv_temp)
+        logits = gram[r, :] * (q_cols[i] * inv_temp) * q_row
+        parts = [logits[:, q] for q in blocks]
+        parts[i] = jnp.where(eye, -1e30, parts[i])
+        logits = jnp.concatenate(parts, axis=1)
+        gram[r, :] = logits
         top = jnp.max(logits, axis=1, keepdims=True)
         sum_exp = jnp.sum(jnp.exp(logits - top), axis=1, keepdims=True)
         lse = top + jnp.log(sum_exp)
@@ -348,21 +370,24 @@
         loss = loss + jnp.sum(lse - at_pos, axis=0, keepdims=True)
         lse_cols.append(lse)
     loss_ref[...] = jnp.broadcast_to(loss * (1.0 / ALL), (1, 128))
-    lse_row = as_row(lse_cols)
-
+
+    factor = inv_temp * (1.0 / ALL)
+    shift_cols = [lse - jnp.log(jnp.broadcast_to(factor, (RB, 1))) for lse in lse_cols]
+    shift_row = as_row(shift_cols)
     for i, r in enumerate(blocks):
-        cosine = gram[r, :]
-        diagonal = lane_all == sub_all + i * RB
-        logits = jnp.where(diagonal, -1e30, cosine * inv_temp)
-        factor = inv_temp * (1.0 / ALL)
-        own = (jnp.exp(logits - lse_cols[i]) - (lane_all == pos_col[r]).astype(F32)) * factor
-        other = (jnp.exp(logits - lse_row) - (sub_all + i * RB == pos_row).astype(F32)) * factor
+        logits = gram[r, :]
+        own = jnp.exp(logits - shift_cols[i])
+        own = jnp.where(lane_all == pos_col[r], own - factor, own)
+        other = jnp.exp(logits - shift_row)
+        other = jnp.where(sub_all == pos_row - i * RB, other - factor, other)
         both = own.astype(BF16).astype(F32) + other.astype(BF16).astype(F32)
-        along = jnp.sum(both * cosine, axis=1, keepdims=True)
-        grads = (both - jnp.where(diagonal, along, 0.0)) * q_cols[i] * q_row
+        along = jnp.sum(both * logits, axis=1, keepdims=True) * (1.0 / inv_temp)
+        parts = [both[:, q] for q in blocks]
+        parts[i] = jnp.where(eye, -along, parts[i])
+        grads = jnp.concatenate(parts, axis=1) * q_cols[i] * q_row
         gram[r, :] = grads
         if i < 2:
-            grads = jnp.where(lane_all < HALF, grads, 2.0 * grads)
+            grads = jnp.concatenate([grads[:, 0:HALF], 2.0 * grads[:, HALF:]], axis=1)
         nmat[r, :] = grads.astype(BF16)
 
     n_own = gram[pl.ds(pl.multiple_of(dp * DOCS, DOCS), DOCS), :]
@@ -402,17 +427,19 @@
 
 def final_kernel(h_ref, gd_ref, oh_ref, sc_ref, gg_ref, loss_ref, out_hbm, gg_out, loss_out, grad, out, sem):
     select = oh_ref[:, 0:2 * DOCS]
+    acc = jnp.zeros((TOK, 128), F32)
     for j in range(D // FB):
         cols = slice(j * FB, (j + 1) * FB)
-        grad[:, cols] = dot(select, gd_ref[:, cols], ((1,), (0,)))
+        rows = dot(select, gd_ref[:, cols], ((1,), (0,)))
+        grad[:, cols] = rows
+        rows = rows * h_ref[:, cols].astype(F32)
+        for k in range(FB // 128):
+            acc = acc + rows[:, k * 128:(k + 1) * 128]
+    inner_all = jnp.sum(acc, axis=1, keepdims=True) * (1.0 / D)
     copies = []
     for i in range(TOK // ROWS):
         r = slice(i * ROWS, (i + 1) * ROWS)
-        acc = jnp.zeros((ROWS, 128), F32)
-        for j in range(D // 128):
-            cols = slice(j * 128, (j + 1) * 128)
-            acc = acc + grad[r, cols] * h_ref[r, cols].astype(F32)
-        inner = jnp.sum(acc, axis=1, keepdims=True) * (1.0 / D)
+        inner = inner_all[r]
         scale = sc_ref[r, 0:1]
         coef = scale * scale * scale * inner
         for j in range(D // 512):

time: 48 us -> 46.6 us (0.971)
  Pallas kernels: 46.6 us -> 45.1 us
    pallas_call x1, Pallas kernels: 43.6 us -> 42.2 us  [body(): pl.pallas_call(gather_kernel, name='pool_gather', out_shape=(jax.ShapeDty...]
where the time goes in v4:
time: 46.6 us; the launch traced here: 46.4 us
  Pallas kernels  45.1 us (97%)
  between operations  1.29 us (3%)
    pallas_call x1, Pallas kernels, body(): pl.pallas_call(gather_kernel, name='pool_gather', out_shape=(jax.ShapeDty...  42.2 us
    pallas_call x1, Pallas kernels, body(): pl.pallas_call(final_kernel, name='grad_hidden', out_shape=(jax.ShapeDtyp...  2.96 us

profile of v4, /device:TPU:1, one launch (start us, length us, event | category | flops | bytes accessed | tf_op | source)
XLA Modules:
  0.0 46.4 jit_solution(481914108728497150)
XLA Ops:
  1.3 42.2 %pool_gather.1 = (bf16[32,4096]{1,0:T(8,128)(2,1)S(1)}, bf16[256,128]{1,0:T(8,128)(2,1)S(1)}, f32[256,128]{1,0:T(8,128)S(1)}, f32[1,4096]{1,0:T(1,128)S(1)}, f32...) custom-call(bf16[256,4096]{1,0:T(8,128)(2,1)} %bitcast.7, s32[1,256]{1,0:T(1,128)} %seg_hbm.1, s32[2]{0:T(128)} %pos_ref.1, ...), custom_call_target="tpu_custom_call" | custom-call | tf_op jit(solution)/shard_map/pool_gather/pallas_call | solution.py:462
  43.5 3.0 %grad_hidden.1 = (bf16[1,256,4096]{2,1,0:T(8,128)(2,1)}, f32[1,4096]{1,0:T(1,128)}, f32[1,128]{1,0:T(1,128)}) custom-call(bf16[256,4096]{1,0:T(8,128)(2,1)S(1)} %get-tuple-element.12.h_ref, bf16[32,4096]{1,0:T(8,128)(2,1)S(1)} %get-tuple-element.13.gd_ref, bf16[256,128]{1,0:T(8,128)(2,1)S(1)} %get-tuple-element.14.oh_ref, ...), custom_call_target="tpu_custom_call" | custom-call | tf_op jit(solution)/shard_map/grad_hidden/pallas_call | solution.py:494

commit v5 on v4

--- a/solution.py
+++ b/solution.py
@@ -20,7 +20,7 @@
 FB = D // N_CTX
 HALF = ALL // 2
 ROWS = 32
-DIRECT = (3, 4)
+DIRECT = (4,)
 RB = 128
 
 
@@ -119,16 +119,11 @@
     pl.semaphore_wait(barrier, len(peers))
     others = [mod(ctx + k, N_CTX) for k in (4, 5, 3, 2, 6, 7, 1)]
     for other in others:
+        m1(ctx, other).start()
+    for other in others:
         p1(ctx, other).start()
-    for other in others:
-        m1(ctx, other).start()
 
     my_col = pl.ds(pl.multiple_of(ctx * FB, FB), FB)
-    total = part[:, my_col].astype(F32)
-    for other in reversed(others):
-        p1(other, ctx).wait_recv()
-        total = total + recv[other].astype(F32)
-    emb[dp, :, my_col] = total.astype(BF16)
 
     def zcopy(zz, dst):
         ref = emb.at[x * NZ + zz, :, my_col]
@@ -218,93 +213,121 @@
             acopy(0, g, way, a_off(k)).start()
         spread(0, g)
 
-    def along_a(g):
-        for way, k in ((0, 3), (1, 1), (2, 2)):
-            acopy(k, g, way, a).wait_recv()
-            spread(k, g)
-
-    def relay(am, g):
-        bcopy(am, 3, g, 0, b).wait_recv()
-        bcopy(am, 1, g, 1, b).wait_recv()
-        if g in DIRECT:
-            pass
-        elif (g + (am >= 2)) % 2 == 0:
-            bcopy(am, 3, g, 2, b_off(1)).start()
-        else:
-            bcopy(am, 1, g, 2, b_off(3)).start()
-        sib(am, 3, g)
-        sib(am, 1, g)
+    def from_a(am, g):
+        acopy(am, g, {3: 0, 1: 1, 2: 2}[am], a).wait_recv()
+        spread(am, g)
+
+    def from_b(am, bm, g):
+        bcopy(am, bm, g, 0 if bm == 3 else 1, b).wait_recv()
+        if g not in DIRECT and bm == (3 if (g + (am >= 2)) % 2 == 0 else 1):
+            bcopy(am, bm, g, 2, b_off(4 - bm)).start()
+        sib(am, bm, g)
 
     def last(am, g):
         bcopy(am, 2, g, 2, b).wait_recv()
         sib(am, 2, g)
 
-    z_own(zcopy)
-    enter(0)
     meta_sum = meta_own[...]
-    for other in others:
+    for other in reversed(others):
         m1(other, ctx).wait_recv()
         meta_sum = meta_sum + meta_ctx[other]
     meta[dp] = meta_sum
     z_own(mz)
+    total = part[:, my_col].astype(F32)
+    for other in reversed(others):
+        p1(other, ctx).wait_recv()
+        total = total + recv[other].astype(F32)
+    emb[dp, :, my_col] = total.astype(BF16)
+    z_own(zcopy)
+    enter(0)
+    from_a(3, 0)
+    from_a(1, 0)
     z_near(zcopy)
+    z_near(mz)
     enter(1)
-    z_near(mz)
-    along_a(0)
-    relay(0, 0)
+    from_b(0, 3, 0)
+    from_b(0, 1, 0)
+    from_a(2, 0)
     z_next(zcopy)
+    z_next(mz)
     enter(2)
-    z_next(mz)
-    along_a(1)
+    from_b(3, 3, 0)
+    from_b(3, 1, 0)
+    from_b(1, 3, 0)
+    from_b(1, 1, 0)
+    from_a(3, 1)
+    from_a(1, 1)
+    from_b(0, 1, 1)
     z_far(zcopy, (3, -3))
     enter(3)
-    relay(0, 1)
-    along_a(2)
+    from_b(0, 3, 1)
+    from_b(2, 1, 0)
+    last(0, 0)
+    from_b(2, 3, 0)
+    from_a(2, 1)
+    from_a(1, 2)
+    from_a(3, 2)
+    from_b(0, 3, 2)
+    last(1, 0)
+    from_b(3, 3, 1)
     z_far(zcopy, (4,))
     enter(4)
     z_far(mz, (3, -3, 4))
     for k in range(1, NX):
         mx(x, mod(x + k, NX)).start()
-    relay(3, 0)
-    relay(1, 0)
-    relay(2, 0)
-    along_a(3)
-    relay(0, 2)
-    last(0, 0)
-    along_a(4)
-    relay(3, 1)
-    relay(1, 1)
-    relay(2, 1)
+    from_b(0, 1, 2)
+    from_b(1, 3, 1)
     last(3, 0)
-    last(1, 0)
+    from_a(2, 2)
+    from_b(3, 1, 1)
+    from_a(3, 3)
+    from_b(1, 1, 1)
+    last(0, 1)
+    from_a(1, 3)
+    from_b(0, 1, 3)
+    from_b(0, 3, 3)
     last(2, 0)
-    relay(0, 3)
-    last(0, 1)
-    relay(3, 2)
-    relay(1, 2)
-    relay(2, 2)
-    relay(0, 4)
+    from_b(2, 3, 1)
+    from_a(2, 3)
+    from_b(2, 1, 1)
+    from_b(1, 3, 2)
+    from_b(1, 1, 2)
+    from_b(3, 3, 2)
+    from_b(3, 1, 2)
+    last(0, 2)
+    from_a(1, 4)
     last(3, 1)
+    from_a(3, 4)
+    from_b(0, 3, 4)
+    from_b(0, 1, 4)
+    from_b(2, 3, 2)
+    from_a(2, 4)
+    from_b(3, 3, 3)
+    from_b(1, 3, 3)
+    last(2, 1)
+    from_b(2, 1, 2)
+    last(0, 4)
+    from_b(2, 3, 3)
+    from_b(3, 1, 3)
     last(1, 1)
-    last(2, 1)
-    last(0, 2)
-    relay(3, 3)
-    relay(1, 3)
-    relay(2, 3)
-    relay(3, 4)
-    relay(1, 4)
-    relay(2, 4)
+    last(1, 2)
+    from_b(1, 1, 3)
+    from_b(1, 3, 4)
+    last(0, 3)
+    from_b(2, 1, 3)
     last(3, 2)
-    last(1, 2)
+    from_b(3, 3, 4)
+    from_b(1, 1, 4)
+    last(1, 4)
+    from_b(3, 1, 4)
+    from_b(2, 1, 4)
+    from_b(2, 3, 4)
+    last(3, 4)
+    last(3, 3)
+    last(2, 3)
     last(2, 2)
-    last(0, 3)
-    last(3, 3)
+    last(2, 4)
     last(1, 3)
-    last(2, 3)
-    last(0, 4)
-    last(3, 4)
-    last(1, 4)
-    last(2, 4)
 
     def gram_of(core, first_time):
         for yy in range(NY):

time: 46.6 us -> 46 us (0.987)
  Pallas kernels: 45.1 us -> 44.6 us
    pallas_call x1, Pallas kernels: 42.2 us -> 41.6 us  [body(): pl.pallas_call(gather_kernel, name='pool_gather', out_shape=(jax.ShapeDty...]
where the time goes in v5:
time: 46 us; the launch traced here: 45.9 us
  Pallas kernels  44.6 us (97%)
  between operations  1.29 us (3%)
    pallas_call x1, Pallas kernels, body(): pl.pallas_call(gather_kernel, name='pool_gather', out_shape=(jax.ShapeDty...  41.6 us
    pallas_call x1, Pallas kernels, body(): pl.pallas_call(final_kernel, name='grad_hidden', out_shape=(jax.ShapeDtyp...  2.96 us

profile of v5, /device:TPU:1, one launch (start us, length us, event | category | flops | bytes accessed | tf_op | source)
XLA Modules:
  0.0 45.9 jit_solution(1760723059851495809)
XLA Ops:
  1.3 41.6 %pool_gather.1 = (bf16[32,4096]{1,0:T(8,128)(2,1)S(1)}, bf16[256,128]{1,0:T(8,128)(2,1)S(1)}, f32[256,128]{1,0:T(8,128)S(1)}, f32[1,4096]{1,0:T(1,128)S(1)}, f32...) custom-call(bf16[256,4096]{1,0:T(8,128)(2,1)} %bitcast.7, s32[1,256]{1,0:T(1,128)} %seg_hbm.1, s32[2]{0:T(128)} %pos_ref.1, ...), custom_call_target="tpu_custom_call" | custom-call | tf_op jit(solution)/shard_map/pool_gather/pallas_call | solution.py:485
  42.9 3.0 %grad_hidden.1 = (bf16[1,256,4096]{2,1,0:T(8,128)(2,1)}, f32[1,4096]{1,0:T(1,128)}, f32[1,128]{1,0:T(1,128)}) custom-call(bf16[256,4096]{1,0:T(8,128)(2,1)S(1)} %get-tuple-element.12.h_ref, bf16[32,4096]{1,0:T(8,128)(2,1)S(1)} %get-tuple-element.13.gd_ref, bf16[256,128]{1,0:T(8,128)(2,1)S(1)} %get-tuple-element.14.oh_ref, ...), custom_call_target="tpu_custom_call" | custom-call | tf_op jit(solution)/shard_map/grad_hidden/pallas_call | solution.py:517

commit v6 on v5

--- a/solution.py
+++ b/solution.py
@@ -20,7 +20,7 @@
 FB = D // N_CTX
 HALF = ALL // 2
 ROWS = 32
-DIRECT = (4,)
+DIRECT = (5, 6, 7)
 RB = 128
 
 
@@ -148,9 +148,8 @@
 
     odd = mod(z, 2)
     z_off = lambda k: mod(z + k + NZ, NZ)
-    pair_off = lambda k: 2 * mod(lax.div(z, 2) + k, NZ // 2)
-    first = [z, z + 1 - 2 * odd, pair_off(3 - 2 * odd), pair_off(1 + 2 * odd), pair_off(2)]
-    size = [1, 1, 2, 2, 2]
+    first = [z, z_off(1), z_off(-1), z_off(2), z_off(-2), z_off(3), z_off(-3), z_off(4)]
+    size = [1] * NZ
 
     def z_own(copy):
         for k in (1, -1, 2, -2):
@@ -242,92 +241,140 @@
     enter(0)
     from_a(3, 0)
     from_a(1, 0)
+    from_b(0, 3, 0)
     z_near(zcopy)
     z_near(mz)
     enter(1)
-    from_b(0, 3, 0)
+    enter(2)
     from_b(0, 1, 0)
     from_a(2, 0)
     z_next(zcopy)
     z_next(mz)
-    enter(2)
+    enter(3)
+    enter(4)
     from_b(3, 3, 0)
     from_b(3, 1, 0)
     from_b(1, 3, 0)
     from_b(1, 1, 0)
+    last(0, 0)
+    from_a(1, 1)
     from_a(3, 1)
-    from_a(1, 1)
     from_b(0, 1, 1)
+    from_a(1, 2)
     z_far(zcopy, (3, -3))
-    enter(3)
+    enter(5)
+    enter(6)
     from_b(0, 3, 1)
+    from_a(3, 2)
+    from_b(0, 1, 2)
+    from_b(0, 3, 2)
     from_b(2, 1, 0)
-    last(0, 0)
+    from_a(2, 1)
     from_b(2, 3, 0)
-    from_a(2, 1)
-    from_a(1, 2)
-    from_a(3, 2)
-    from_b(0, 3, 2)
-    last(1, 0)
-    from_b(3, 3, 1)
+    from_a(1, 3)
+    from_a(2, 2)
+    from_a(3, 3)
+    from_b(0, 1, 3)
+    from_a(1, 4)
+    from_b(0, 3, 3)
+    from_a(3, 4)
+    from_b(0, 1, 4)
     z_far(zcopy, (4,))
-    enter(4)
+    enter(7)
     z_far(mz, (3, -3, 4))
     for k in range(1, NX):
         mx(x, mod(x + k, NX)).start()
-    from_b(0, 1, 2)
+    from_b(0, 3, 4)
+    last(3, 0)
+    from_a(2, 3)
+    last(1, 0)
+    from_b(1, 1, 1)
+    from_a(2, 4)
     from_b(1, 3, 1)
-    last(3, 0)
-    from_a(2, 2)
     from_b(3, 1, 1)
-    from_a(3, 3)
-    from_b(1, 1, 1)
+    from_b(3, 3, 1)
     last(0, 1)
-    from_a(1, 3)
-    from_b(0, 1, 3)
-    from_b(0, 3, 3)
+    from_b(1, 3, 2)
+    from_b(1, 1, 2)
+    from_a(3, 5)
+    from_a(1, 5)
+    from_b(0, 1, 5)
+    from_a(1, 6)
+    from_b(0, 3, 5)
+    from_b(0, 1, 6)
+    from_a(2, 5)
+    from_a(3, 6)
+    from_b(0, 3, 6)
+    from_a(2, 6)
+    from_b(3, 3, 2)
+    from_b(3, 1, 2)
+    last(0, 5)
+    last(0, 2)
     last(2, 0)
     from_b(2, 3, 1)
-    from_a(2, 3)
     from_b(2, 1, 1)
-    from_b(1, 3, 2)
-    from_b(1, 1, 2)
-    from_b(3, 3, 2)
-    from_b(3, 1, 2)
-    last(0, 2)
-    from_a(1, 4)
+    last(0, 6)
+    from_b(1, 3, 3)
+    from_b(1, 1, 3)
+    from_b(2, 3, 2)
+    from_b(2, 1, 2)
+    from_b(3, 3, 3)
+    from_b(3, 1, 3)
+    last(0, 3)
+    from_b(1, 3, 4)
+    from_b(1, 1, 4)
+    from_b(3, 3, 4)
+    from_b(3, 1, 4)
+    from_a(3, 7)
+    from_a(1, 7)
+    from_b(0, 1, 7)
+    from_b(0, 3, 7)
+    from_b(2, 1, 3)
+    last(1, 1)
+    from_b(2, 1, 4)
+    from_a(2, 7)
+    last(0, 4)
+    from_b(3, 1, 5)
+    from_b(2, 3, 3)
+    from_b(2, 3, 4)
+    last(0, 7)
     last(3, 1)
-    from_a(3, 4)
-    from_b(0, 3, 4)
-    from_b(0, 1, 4)
-    from_b(2, 3, 2)
-    from_a(2, 4)
-    from_b(3, 3, 3)
-    from_b(1, 3, 3)
+    from_b(1, 1, 5)
+    last(1, 2)
+    from_b(3, 3, 5)
+    last(3, 5)
+    from_b(1, 3, 5)
+    from_b(1, 1, 6)
+    from_b(1, 3, 6)
+    from_b(2, 1, 5)
+    from_b(3, 1, 6)
+    last(1, 5)
+    from_b(2, 1, 6)
+    from_b(2, 3, 5)
+    last(3, 2)
+    last(1, 6)
+    from_b(3, 3, 6)
+    last(1, 3)
+    last(2, 2)
+    last(2, 6)
+    last(3, 4)
+    last(2, 5)
+    from_b(2, 3, 6)
+    from_b(3, 1, 7)
     last(2, 1)
-    from_b(2, 1, 2)
-    last(0, 4)
-    from_b(2, 3, 3)
-    from_b(3, 1, 3)
-    last(1, 1)
-    last(1, 2)
-    from_b(1, 1, 3)
-    from_b(1, 3, 4)
-    last(0, 3)
-    from_b(2, 1, 3)
-    last(3, 2)
-    from_b(3, 3, 4)
-    from_b(1, 1, 4)
+    last(3, 3)
+    last(3, 6)
     last(1, 4)
-    from_b(3, 1, 4)
-    from_b(2, 1, 4)
-    from_b(2, 3, 4)
-    last(3, 4)
-    last(3, 3)
+    from_b(1, 1, 7)
+    from_b(3, 3, 7)
+    from_b(1, 3, 7)
+    last(3, 7)
+    last(2, 4)
+    from_b(2, 3, 7)
+    from_b(2, 1, 7)
+    last(1, 7)
     last(2, 3)
-    last(2, 2)
-    last(2, 4)
-    last(1, 3)
+    last(2, 7)
 
     def gram_of(core, first_time):
         for yy in range(NY):
@@ -509,7 +556,7 @@
             dma((2,)),
             dma((4,)),
             dma, dma((N_CTX,)), dma, dma((NZ,)), dma, dma((NX,)), dma, dma((N_CTX,)),
-            dma, dma((NZ,)), dma, dma((15,)), dma, dma((60,)), dma, dma,
+            dma, dma((NZ,)), dma, dma((24,)), dma, dma((96,)), dma, dma,
         ],
         compiler_params=pltpu.CompilerParams(collective_id=0, has_side_effects=True, vmem_limit_bytes=20 << 20),
     )(hbm(hidden[0]), hbm(segments), hbm(positives), hbm(gain.reshape(1, D)), inv_temp.reshape(1))

time: 46 us -> 45.2 us (0.983)
  Pallas kernels: 44.6 us -> 43.8 us
    pallas_call x1, Pallas kernels: 41.6 us -> 40.9 us  [body(): pl.pallas_call(gather_kernel, name='pool_gather', out_shape=(jax.ShapeDty...]
where the time goes in v6:
time: 45.2 us; the launch traced here: 45.1 us
  Pallas kernels  43.8 us (97%)
  between operations  1.29 us (3%)
    pallas_call x1, Pallas kernels, body(): pl.pallas_call(gather_kernel, name='pool_gather', out_shape=(jax.ShapeDty...  40.9 us
    pallas_call x1, Pallas kernels, body(): pl.pallas_call(final_kernel, name='grad_hidden', out_shape=(jax.ShapeDtyp...  2.96 us

profile of v6, /device:TPU:1, one launch (start us, length us, event | category | flops | bytes accessed | tf_op | source)
XLA Modules:
  0.0 45.1 jit_solution(1016063749074109249)
XLA Ops:
  1.3 40.9 %pool_gather.1 = (bf16[32,4096]{1,0:T(8,128)(2,1)S(1)}, bf16[256,128]{1,0:T(8,128)(2,1)S(1)}, f32[256,128]{1,0:T(8,128)S(1)}, f32[1,4096]{1,0:T(1,128)S(1)}, f32...) custom-call(bf16[256,4096]{1,0:T(8,128)(2,1)} %bitcast.7, s32[1,256]{1,0:T(1,128)} %seg_hbm.1, s32[2]{0:T(128)} %pos_ref.1, ...), custom_call_target="tpu_custom_call" | custom-call | tf_op jit(solution)/shard_map/pool_gather/pallas_call | solution.py:532
  42.1 3.0 %grad_hidden.1 = (bf16[1,256,4096]{2,1,0:T(8,128)(2,1)}, f32[1,4096]{1,0:T(1,128)}, f32[1,128]{1,0:T(1,128)}) custom-call(bf16[256,4096]{1,0:T(8,128)(2,1)S(1)} %get-tuple-element.12.h_ref, bf16[32,4096]{1,0:T(8,128)(2,1)S(1)} %get-tuple-element.13.gd_ref, bf16[256,128]{1,0:T(8,128)(2,1)S(1)} %get-tuple-element.14.oh_ref, ...), custom_call_target="tpu_custom_call" | custom-call | tf_op jit(solution)/shard_map/grad_hidden/pallas_call | solution.py:564

commit v7 on v6

--- a/solution.py
+++ b/solution.py
@@ -394,12 +394,8 @@
         src_ref=emb.at[pl.ds(0, N_DP // 2)], dst_ref=emb.at[pl.ds(0, N_DP // 2)],
         send_sem=s_send, recv_sem=s_recv, device_id=sibling, device_id_type=MESH,
     ).wait_recv()
-    gram_of(1 - c, False)
-    gram[HALF:, 0:HALF] = jnp.transpose(gram[0:HALF, HALF:])
-
     for k in range(1, NX):
         mx(mod(x + k, NX), x).wait_recv()
-
     inv_temp = it_ref[0]
     info = jnp.broadcast_to(meta[...], (N_DP, DOCS, 128)).reshape(ALL, 128)
     at = lax.broadcasted_iota(jnp.int32, (ALL, 128), 1) - mod(lax.broadcasted_iota(jnp.int32, (ALL, 128), 0), DOCS)
@@ -414,6 +410,11 @@
             [jnp.sum(jnp.where(eye, jnp.broadcast_to(v, (RB, RB)), 0.0), axis=0, keepdims=True) for v in cols],
             axis=1,
         )
+    pos_row = as_row([pos_f[r] for r in blocks]).astype(jnp.int32)
+
+    gram_of(1 - c, False)
+    gram[HALF:, 0:HALF] = jnp.transpose(gram[0:HALF, HALF:])
+
 
     q_cols = []
     for r in blocks:
@@ -421,7 +422,6 @@
         inv_count = 1.0 / count_col[r]
         q_cols.append(inv_count * lax.rsqrt(norm2 * inv_count * inv_count + 1e-06))
     q_row = as_row(q_cols)
-    pos_row = as_row([pos_f[r] for r in blocks]).astype(jnp.int32)
 
     lane_all = lax.broadcasted_iota(jnp.int32, (RB, ALL), 1)
     sub_all = lax.broadcasted_iota(jnp.int32, (RB, ALL), 0)

time: 45.2 us -> 45.1 us (level)
  no operation moved by 1% of the time
where the time goes in v7:
time: 45.1 us; the launch traced here: 45 us
  Pallas kernels  43.7 us (97%)
  between operations  1.29 us (3%)
    pallas_call x1, Pallas kernels, body(): pl.pallas_call(gather_kernel, name='pool_gather', out_shape=(jax.ShapeDty...  40.7 us
    pallas_call x1, Pallas kernels, body(): pl.pallas_call(final_kernel, name='grad_hidden', out_shape=(jax.ShapeDtyp...  2.96 us

profile of v7, /device:TPU:1, one launch (start us, length us, event | category | flops | bytes accessed | tf_op | source)
XLA Modules:
  0.0 45.0 jit_solution(12501627996660359093)
XLA Ops:
  1.3 40.7 %pool_gather.1 = (bf16[32,4096]{1,0:T(8,128)(2,1)S(1)}, bf16[256,128]{1,0:T(8,128)(2,1)S(1)}, f32[256,128]{1,0:T(8,128)S(1)}, f32[1,4096]{1,0:T(1,128)S(1)}, f32...) custom-call(bf16[256,4096]{1,0:T(8,128)(2,1)} %bitcast.7, s32[1,256]{1,0:T(1,128)} %seg_hbm.1, s32[2]{0:T(128)} %pos_ref.1, ...), custom_call_target="tpu_custom_call" | custom-call | tf_op jit(solution)/shard_map/pool_gather/pallas_call | solution.py:532
  42.0 3.0 %grad_hidden.1 = (bf16[1,256,4096]{2,1,0:T(8,128)(2,1)}, f32[1,4096]{1,0:T(1,128)}, f32[1,128]{1,0:T(1,128)}) custom-call(bf16[256,4096]{1,0:T(8,128)(2,1)S(1)} %get-tuple-element.12.h_ref, bf16[32,4096]{1,0:T(8,128)(2,1)S(1)} %get-tuple-element.13.gd_ref, bf16[256,128]{1,0:T(8,128)(2,1)S(1)} %get-tuple-element.14.oh_ref, ...), custom_call_target="tpu_custom_call" | custom-call | tf_op jit(solution)/shard_map/grad_hidden/pallas_call | solution.py:564
